TPU v7x, 32 devices: a whole 2x2x4 slice. The times are simulated.
32 devices in a mesh: bx: 4 (over z), by: 8 (over y, x, core).
Axes of the slice: x: 2, y: 2, z: 4, core: 2. Of those that a mesh axis runs over, the one named last changes fastest.
Arguments:
- field_now: float32 [4, 64, 256, 256], P(None, 'bx', 'by'), may hold values from -6 to 6
- field_before: float32 [4, 64, 256, 256], P(None, 'bx', 'by'), may hold values from -6 to 6
- interp_weight: bfloat16 [4096, 512, 128], P(('bx', 'by')), may hold values from -0.25 to 0.25
- tile_index: int32 [4096], P(('bx', 'by')), may hold values from 0 to 255
- step_offset: int32 [4096], P(('bx', 'by')), may hold values from 0 to 3
- block_patch: int32 [4096], P(('bx', 'by')), may hold values from 0 to 2047, as said below
- ownership: int32 [2048], replicated, may hold values from 0 to 2047, as said below
- near_pairs: int32 [4096, 2], P(('bx', 'by')), may hold values from 0 to 63
- precorrection: bfloat16 [4096, 128, 128], P(('bx', 'by')), may hold values from -0.375 to 0.375
Outputs:
- patch_field: float32 [2048, 4, 128], P(('bx', 'by'))
Inputs may be any that keep to these rules, and one draw needn't show every extreme that they name: `ownership`: a permutation; patch p is owned by device ownership[p] // 64 (device index bx * 8 + by) as its local patch ownership[p] % 64. `block_patch`: the blocks of one device feed at most 8 patches counted with repetition of any one owner; some owner receives exactly 8 blocks from every device.
All inputs are finite; a program needn't handle non-finite values.
Results may differ from a plain program's by a relative error of at most 0.0035.
Values sent between devices are 32-bit elements; how exact they have to be, the bound alone decides.
No kernel may reach another device: no remote copies, remote signals or barrier semaphores. Data moves between devices by JAX's collectives and lax.ppermute only.
A program may use at most 128 MiB of HBM per device.

v0:
```python
import functools

import jax
import jax.numpy as jnp
from jax import lax
from jax.experimental import pallas as pl
from jax.experimental.pallas import tpu as pltpu
from jax.sharding import PartitionSpec as P

STEPS = 4
COEF = 0.3
LANES = 128
TILE = 8
OWN = 8
MEGA = 1 << 20


def ceil8(n):
    return (n + 7) // 8 * 8


def edge_rows():
    at_low = lax.axis_index("by") == 0
    at_high = lax.axis_index("by") == lax.axis_size("by") - 1
    row = lax.broadcasted_iota(jnp.int32, (8, LANES), 0)
    keep_low = row >= jnp.where(at_low, STEPS, 0)
    keep_high = row < jnp.where(at_high, 8 - STEPS, 8)
    return keep_low, keep_high


def beside_z(mid):
    halves = len(mid)
    lane = lax.broadcasted_iota(jnp.int32, mid[0].shape, 1)
    first = lane == 0
    last = lane == LANES - 1
    up = [pltpu.roll(m, 1, 1) for m in mid]
    down = [pltpu.roll(m, LANES - 1, 1) for m in mid]
    sums = []
    for h in range(halves):
        below = jnp.where(first, up[h - 1] if h else 0.0, up[h])
        above = jnp.where(last, down[h + 1] if h + 1 < halves else 0.0, down[h])
        sums.append(below + above)
    return sums


def rows_of(ref, h, c, slot, rows):
    return ref[h, c, slot, OWN - STEPS : OWN - STEPS + rows, :]


def advance(cur, old, c, slot, beside, edges, rows, keep=None):
    halves = cur.shape[0]
    start = OWN - STEPS
    mid = [cur[h, c, slot, start : start + rows, :] for h in range(halves)]
    across = beside_z(mid)
    for h in range(halves):
        total = across[h] + cur[h, c, slot, start - 1 : start - 1 + rows, :]
        total = total + cur[h, c, slot, start + 1 : start + 1 + rows, :]
        for ref, place in beside:
            total = total + rows_of(ref, h, c, place, rows)
        fresh = (2.0 - 6.0 * COEF) * mid[h] - rows_of(old, h, c, slot, rows) + COEF * total
        if keep is not None:
            fresh = jnp.where(keep, fresh, 0.0)
        old[h, c, slot, start : start + 8, :] = jnp.where(edges[0], fresh[:8], 0.0)
        old[h, c, slot, start + 8 : start + rows - 8, :] = fresh[8 : rows - 8]
        old[h, c, slot, start + rows - 8 : start + rows, :] = jnp.where(
            edges[1], fresh[rows - 8 :], 0.0
        )


def fill_rows(now, before, c, slot, y_low, y_high, x, size_y):
    for h in range(now.shape[0]):
        z = slice(h * LANES, (h + 1) * LANES)
        top = OWN + size_y
        now[h, c, slot, OWN - STEPS : OWN, :] = y_low[c, x, :STEPS, z]
        before[h, c, slot, OWN - STEPS : OWN, :] = y_low[c, x, STEPS:, z]
        now[h, c, slot, top : top + STEPS, :] = y_high[c, x, :STEPS, z]
        before[h, c, slot, top : top + STEPS, :] = y_high[c, x, STEPS:, z]


def faces_kernel(now, before, y_low, y_high, out_low, out_high, p_now, p_before, sems, *, size_y):
    comps, size_x, _, size_z = now.shape
    halves = size_z // LANES
    rows = size_y + 2 * STEPS
    near = STEPS
    copies = []
    for a, (src, dst) in enumerate(((now, p_now), (before, p_before))):
        for face in range(2):
            x0 = 0 if face == 0 else size_x - near
            s0 = 2 if face == 0 else 6
            for h in range(halves):
                copies.append(
                    pltpu.make_async_copy(
                        src.at[:, x0 : x0 + near, :, h * LANES : (h + 1) * LANES],
                        dst.at[h, :, s0 : s0 + near, OWN : OWN + size_y, :],
                        sems.at[a, face, h],
                    )
                )
    for copy in copies:
        copy.start()

    def slot(face, depth):
        return depth + 2 if face == 0 else 9 - depth

    edges = edge_rows()
    outs = (out_low, out_high)

    def prepare(c, carry):
        for face in range(2):
            for depth in range(near):
                x = depth if face == 0 else size_x - 1 - depth
                fill_rows(p_now, p_before, c, slot(face, depth), y_low, y_high, x, size_y)
            for depth in (-1, -2):
                for h in range(halves):
                    zero = jnp.zeros((rows + 8, LANES), jnp.float32)
                    p_now[h, c, slot(face, depth)] = zero
                    p_before[h, c, slot(face, depth)] = zero
        return carry

    lax.fori_loop(0, comps, prepare, 0)
    for copy in copies:
        copy.wait()

    def give(buf, c, step, offset):
        more = STEPS - 1 - step
        for face in range(2):
            place = slot(face, 0)
            for h in range(halves):
                outs[face][c, h, step * size_y : (step + 1) * size_y, :] = buf[
                    h, c, place, OWN : OWN + size_y, :
                ]
                if more:
                    base = STEPS * size_y + offset
                    outs[face][c, h, base : base + more, :] = buf[h, c, place, OWN - more : OWN, :]
                    outs[face][c, h, base + more : base + 2 * more, :] = buf[
                        h, c, place, OWN + size_y : OWN + size_y + more, :
                    ]

    def evolve(c, carry):
        cur, old = p_now, p_before
        give(cur, c, 0, 0)
        offset = 2 * (STEPS - 1)
        for step, depths in ((1, (-1, 0, 1, 2)), (2, (-1, 0, 1)), (3, (0,))):
            for face in range(2):
                for depth in depths:
                    place = slot(face, depth)
                    advance(
                        cur, old, c, place, ((cur, place - 1), (cur, place + 1)), edges, rows
                    )
            cur, old = old, cur
            give(cur, c, step, offset)
            offset += 2 * (STEPS - 1 - step)
        for face in range(2):
            for h in range(halves):
                base = STEPS * size_y + offset
                outs[face][c, h, base : base + 4, :] = jnp.zeros((4, LANES), jnp.float32)
        return carry

    lax.fori_loop(0, comps, evolve, 0)


def identity(n, dtype):
    row = lax.broadcasted_iota(jnp.int32, (n, n), 0)
    col = lax.broadcasted_iota(jnp.int32, (n, n), 1)
    return (row == col).astype(jnp.float32).astype(dtype)


def turn_tile(buf, x0, count_x, y0, eye):
    halves, comps = buf.shape[:2]
    parts = []
    for h in range(halves):
        cells = buf[h, :, pl.ds(x0, count_x), pl.ds(y0, TILE), :]
        parts.append(cells.reshape(comps * count_x * TILE, LANES).astype(jnp.bfloat16))
    cells = jnp.concatenate(parts, axis=1)
    return lax.dot_general(
        eye, cells, (((1,), (1,)), ((), ())), preferred_element_type=jnp.float32
    )


def fill_spread(spread, comps, planes):
    rows, cols = spread.shape
    per = planes * TILE * TILE
    for c in range(comps):
        row = lax.broadcasted_iota(jnp.int32, (rows, per), 0)
        col = lax.broadcasted_iota(jnp.int32, (rows, per), 1)
        hot = row == col // TILE + c * planes * TILE
        spread[:, c * per : (c + 1) * per] = hot.astype(jnp.float32).astype(jnp.bfloat16)


def spread_group(table, index, spread, comps, group):
    cells = jnp.concatenate([table[index(b)] for b in range(group)], axis=0)
    wide = jnp.dot(
        cells.astype(jnp.bfloat16), spread[...], preferred_element_type=jnp.float32
    )
    row = lax.broadcasted_iota(jnp.int32, wide.shape, 0) % TILE
    col = lax.broadcasted_iota(jnp.int32, wide.shape, 1) % TILE
    wide = jnp.where(row == col, wide, 0.0)
    per = wide.shape[1] // comps
    return [
        jnp.concatenate(
            [wide[b * TILE : (b + 1) * TILE, c * per : (c + 1) * per] for c in range(comps)],
            axis=0,
        ).astype(jnp.bfloat16)
        for b in range(group)
    ]


GROUP = 8


def own_kernel(
    tile_index, step_offset, now, before, y_low, y_high, weight, out,
    p_now, p_before, table, held, spread, sems, wsems,
):
    comps, size_x, size_y, size_z = now.shape
    halves = size_z // LANES
    rows = size_y + 2 * STEPS
    blocks = weight.shape[0]
    tiles_y = size_y // TILE
    tiles_z = size_z // TILE
    columns = size_x // TILE * tiles_y
    copies = []
    for a, (src, dst) in enumerate(((now, p_now), (before, p_before))):
        for h in range(halves):
            copies.append(
                pltpu.make_async_copy(
                    src.at[:, :, :, h * LANES : (h + 1) * LANES],
                    dst.at[h, :, 2 : 2 + size_x, OWN : OWN + size_y, :],
                    sems.at[a, h],
                )
            )
    for copy in copies:
        copy.start()

    def weights(g):
        part = pl.ds(g * GROUP, GROUP)
        return pltpu.make_async_copy(weight.at[part], held.at[part], wsems.at[g])

    def start(g, carry):
        weights(g).start()
        return carry

    lax.fori_loop(0, blocks // GROUP, start, 0)
    edges = edge_rows()
    keep_low = lax.axis_index("bx") > 0
    keep_high = lax.axis_index("bx") < lax.axis_size("bx") - 1

    def prepare(c, carry):
        def one(x, carry):
            fill_rows(p_now, p_before, c, x + 2, y_low, y_high, x, size_y)
            return carry

        lax.fori_loop(0, size_x, one, 0)
        for place in (0, 1, size_x + 2, size_x + 3):
            for h in range(halves):
                zero = jnp.zeros((rows + 8, LANES), jnp.float32)
                p_now[h, c, place] = zero
                p_before[h, c, place] = zero
        return carry

    lax.fori_loop(0, comps, prepare, 0)
    fill_spread(spread, comps, TILE)
    eye = identity(size_z, jnp.bfloat16)
    for copy in copies:
        copy.wait()
    cur, old = p_now, p_before
    for step in range(STEPS):
        out_planes = (1, 2, 1, 0)[step]

        def evolve(c, carry, cur=cur, old=old, out_planes=out_planes):
            def inner(x, carry):
                place = x + 2
                advance(cur, old, c, place, ((cur, place - 1), (cur, place + 1)), edges, rows)
                return carry

            lax.fori_loop(0, size_x, inner, 0)
            for depth in range(1, out_planes + 1):
                for face in range(2):
                    place = 2 - depth if face == 0 else size_x + 1 + depth
                    inward = place + 1 if face == 0 else place - 1
                    outward = place - 1 if face == 0 else place + 1
                    beside = [(cur, inward)]
                    if depth < 2:
                        beside.append((cur, outward))
                    advance(
                        cur, old, c, place, beside, edges, rows, keep_high if face else keep_low
                    )
            return carry

        lax.fori_loop(0, comps, evolve, 0)

        def turn(column, carry, fresh=old, step=step):
            x0 = 2 + column // tiles_y * TILE
            y0 = OWN + column % tiles_y * TILE
            turned = turn_tile(fresh, x0, TILE, pl.multiple_of(y0, TILE), eye)
            first = (step * columns + column) * tiles_z
            table[pl.ds(first, tiles_z)] = turned.reshape(tiles_z, TILE, comps * TILE * TILE)
            return carry

        lax.fori_loop(0, columns, turn, 0)
        cur, old = old, cur

    def panels(g, carry):
        weights(g).wait()

        def index(b):
            block = g * GROUP + b
            return step_offset[block] * (columns * tiles_z) + tile_index[block]

        lhs = spread_group(table, index, spread, comps, GROUP)
        for b in range(GROUP):
            made = jnp.dot(lhs[b], held[g * GROUP + b], preferred_element_type=jnp.float32)
            for c in range(comps):
                total = jnp.sum(made[c * TILE : (c + 1) * TILE], axis=0, keepdims=True)
                out[pl.ds(g * GROUP * comps + b * comps + c, 1), :] = total
        return carry

    lax.fori_loop(0, blocks // GROUP, panels, 0)


def share_kernel(
    tile_index, step_offset, block_patch, ownership, from_low, from_high, weight, own_panels, out,
    bound, d_now, d_before, table, held, spread, count, wsems,
    *, size_x, size_y, size_z, slots, stride,
):
    comps = from_low.shape[0]
    halves = size_z // LANES
    rows = size_y + 2 * STEPS
    blocks = weight.shape[0]
    tiles_y = size_y // TILE
    tiles_z = size_z // TILE
    columns = 2 * tiles_y
    devices = lax.axis_size("bx") * lax.axis_size("by")
    owned = ownership.shape[0] // devices
    part = STEPS * TILE * TILE

    def weights(b):
        face = tile_index[b] // (tiles_y * tiles_z)
        return pltpu.make_async_copy(
            weight.at[b, pl.ds(pl.multiple_of(face * part, part), part), :],
            held.at[b],
            wsems.at[b],
        )

    def start(b, carry):
        weights(b).start()
        return carry

    lax.fori_loop(0, blocks, start, 0)
    out[...] = jnp.full(out.shape, -1.0, jnp.float32)

    def clear(d, carry):
        count[d] = 0
        return carry

    lax.fori_loop(0, devices, clear, 0)
    edges = edge_rows()
    froms = (from_low, from_high)

    def prepare(c, carry):
        for face in range(2):
            offset = STEPS * size_y
            for step in range(STEPS):
                place = face * STEPS + step
                more = STEPS - 1 - step
                for h in range(halves):
                    src = froms[face]
                    bound[h, c, place, OWN : OWN + size_y, :] = src[
                        c, h, step * size_y : (step + 1) * size_y, :
                    ]
                    if more:
                        bound[h, c, place, OWN - more : OWN, :] = src[
                            c, h, offset : offset + more, :
                        ]
                        bound[h, c, place, OWN + size_y : OWN + size_y + more, :] = src[
                            c, h, offset + more : offset + 2 * more, :
                        ]
                offset += 2 * more
            for place in range(face * STEPS, (face + 1) * STEPS):
                for h in range(halves):
                    zero = jnp.zeros((rows + 8, LANES), jnp.float32)
                    d_now[h, c, place] = zero
                    d_before[h, c, place] = zero
        return carry

    lax.fori_loop(0, comps, prepare, 0)
    fill_spread(spread, comps, STEPS)
    eye = identity(size_z, jnp.bfloat16)

    def slot(face, depth):
        return depth if face == 0 else 2 * STEPS - 1 - depth

    cur, old = d_now, d_before
    for step in range(STEPS):

        def evolve(c, carry, cur=cur, old=old, step=step):
            for face in range(2):
                for depth in range(step + 1):
                    if depth == 0:
                        beside = [(bound, face * STEPS + step)]
                    else:
                        beside = [(cur, slot(face, depth - 1))]
                    if depth + 1 < STEPS:
                        beside.append((cur, slot(face, depth + 1)))
                    advance(cur, old, c, slot(face, depth), beside, edges, rows)
            return carry

        lax.fori_loop(0, comps, evolve, 0)

        def turn(column, carry, fresh=old, step=step):
            x0 = column // tiles_y * STEPS
            y0 = OWN + column % tiles_y * TILE
            turned = turn_tile(fresh, x0, STEPS, pl.multiple_of(y0, TILE), eye)
            first = (step * columns + column) * tiles_z
            table[pl.ds(first, tiles_z)] = turned.reshape(tiles_z, TILE, comps * STEPS * TILE)
            return carry

        lax.fori_loop(0, columns, turn, 0)
        cur, old = old, cur

    def panels(g, carry):
        def index(b):
            block = g * GROUP + b
            return step_offset[block] * (columns * tiles_z) + tile_index[block]

        lhs = spread_group(table, index, spread, comps, GROUP)
        for b in range(GROUP):
            block = g * GROUP + b
            weights(block).wait()
            made = jnp.dot(lhs[b], held[block], preferred_element_type=jnp.float32)
            target = ownership[block_patch[block]]
            owner = target // owned
            local = target - owner * owned
            rank = count[owner]
            count[owner] = rank + 1
            row = owner * stride + rank
            for c in range(comps):
                total = jnp.sum(made[c * TILE : (c + 1) * TILE], axis=0, keepdims=True)
                total = total + own_panels[pl.ds(block * comps + c, 1), :]
                out[pl.ds(row + c * slots, 1), :] = total
            out[pl.ds(row + comps * slots, 1), :] = jnp.full(
                (1, LANES), local.astype(jnp.float32), jnp.float32
            )
        return carry

    lax.fori_loop(0, blocks // GROUP, panels, 0)


PAIRS = 8


def near_kernel(pairs, got, precorrection, out, field, held, sems, *, comps, slots, stride):
    count = precorrection.shape[0]
    senders = got.shape[0] // stride
    owned = out.shape[0] // comps

    def blocks(g):
        part = pl.ds(g * PAIRS, PAIRS)
        return pltpu.make_async_copy(precorrection.at[part], held.at[part], sems.at[g])

    for g in range(count // PAIRS):
        blocks(g).start()
    whole = got[...].reshape(senders, stride, LANES)
    ids = whole[:, comps * slots : (comps + 1) * slots, :].reshape(senders * slots, LANES)
    ids = ids.T[:owned]
    hot = ids == lax.broadcasted_iota(jnp.int32, ids.shape, 0).astype(jnp.float32)
    hot = hot.astype(jnp.float32).astype(jnp.bfloat16)
    for c in range(comps):
        rest = whole[:, c * slots : (c + 1) * slots, :].reshape(senders * slots, LANES)
        total = None
        for _ in range(3):
            piece = rest.astype(jnp.bfloat16)
            rest = rest - piece.astype(jnp.float32)
            part = jnp.dot(hot, piece, preferred_element_type=jnp.float32)
            total = part if total is None else total + part
        field[pl.ds(c, owned, stride=comps), :] = total
        out[pl.ds(c, owned, stride=comps), :] = total

    def group(g, carry):
        blocks(g).wait()
        for b in range(PAIRS):
            k = g * PAIRS + b
            i = pairs[2 * k]
            j = pairs[2 * k + 1]
            source = field[pl.ds(j * comps, comps), :].astype(jnp.bfloat16)
            term = jnp.dot(source, held[k], preferred_element_type=jnp.float32)
            out[pl.ds(i * comps, comps), :] += term
        return carry

    lax.fori_loop(0, count // PAIRS, group, 0)


SMEM = pl.BlockSpec(memory_space=pltpu.SMEM)
VMEM = pl.BlockSpec(memory_space=pltpu.VMEM)
ANY = pl.BlockSpec(memory_space=pl.ANY)


def kernel_params(mib):
    return pltpu.CompilerParams(vmem_limit_bytes=mib * MEGA)


def per_device(
    field_now,
    field_before,
    interp_weight,
    tile_index,
    step_offset,
    block_patch,
    ownership,
    near_pairs,
    precorrection,
):
    comps, size_x, size_y, size_z = field_now.shape
    count_x = lax.axis_size("bx")
    count_y = lax.axis_size("by")
    devices = count_x * count_y
    blocks, cells, points = interp_weight.shape
    capacity = max(2, (2 * blocks + devices - 1) // devices)
    owned = ownership.shape[0] // devices
    halves = size_z // LANES
    rows = size_y + 2 * OWN
    f32, bf16 = jnp.float32, jnp.bfloat16

    def swap(up, down, axis, count):
        forward = [(i, i + 1) for i in range(count - 1)]
        backward = [(b, a) for a, b in forward]
        return lax.ppermute(up, axis, forward), lax.ppermute(down, axis, backward)

    up = jnp.concatenate([field_now[:, :, -STEPS:], field_before[:, :, -STEPS:]], axis=2)
    down = jnp.concatenate([field_now[:, :, :STEPS], field_before[:, :, :STEPS]], axis=2)
    y_low, y_high = swap(up, down, "by", count_y)

    face_rows = STEPS * size_y + ceil8(STEPS * (STEPS - 1) + 4)
    face = jax.ShapeDtypeStruct((comps, halves, face_rows, LANES), f32)
    plane = pltpu.VMEM((halves, comps, 12, rows, LANES), f32)
    give_low, give_high = pl.pallas_call(
        functools.partial(faces_kernel, size_y=size_y),
        out_shape=(face, face),
        in_specs=[ANY, ANY, VMEM, VMEM],
        out_specs=(VMEM, VMEM),
        scratch_shapes=[plane, plane, pltpu.SemaphoreType.DMA((2, 2, halves))],
        compiler_params=kernel_params(32),
    )(field_now, field_before, y_low, y_high)
    from_low, from_high = swap(give_high, give_low, "bx", count_x)

    tiles = size_x // TILE * (size_y // TILE) * (size_z // TILE)
    brick = pltpu.VMEM((halves, comps, size_x + 4, rows, LANES), f32)
    own_panels = pl.pallas_call(
        own_kernel,
        out_shape=jax.ShapeDtypeStruct((blocks * comps, points), f32),
        in_specs=[SMEM, SMEM, ANY, ANY, VMEM, VMEM, ANY],
        out_specs=VMEM,
        scratch_shapes=[
            brick,
            brick,
            pltpu.VMEM((STEPS * tiles, TILE, comps * TILE * TILE), f32),
            pltpu.VMEM((blocks, cells, points), bf16),
            pltpu.VMEM((comps * TILE * TILE, comps * cells), bf16),
            pltpu.SemaphoreType.DMA((2, halves)),
            pltpu.SemaphoreType.DMA((blocks // GROUP,)),
        ],
        compiler_params=kernel_params(52),
    )(tile_index, step_offset, field_now, field_before, y_low, y_high, interp_weight)

    slots = ceil8(capacity)
    stride = (comps + 1) * slots
    thin = pltpu.VMEM((halves, comps, 2 * STEPS, rows, LANES), f32)
    sent = pl.pallas_call(
        functools.partial(
            share_kernel,
            size_x=size_x,
            size_y=size_y,
            size_z=size_z,
            slots=slots,
            stride=stride,
        ),
        out_shape=jax.ShapeDtypeStruct((devices * stride, points), f32),
        in_specs=[SMEM, SMEM, SMEM, SMEM, VMEM, VMEM, ANY, VMEM],
        out_specs=VMEM,
        scratch_shapes=[
            thin,
            thin,
            thin,
            pltpu.VMEM((STEPS * tiles, TILE, comps * STEPS * TILE), f32),
            pltpu.VMEM((blocks, STEPS * TILE * TILE, points), bf16),
            pltpu.VMEM((comps * STEPS * TILE, comps * STEPS * TILE * TILE), bf16),
            pltpu.SMEM((devices,), jnp.int32),
            pltpu.SemaphoreType.DMA((blocks,)),
        ],
        compiler_params=kernel_params(52),
    )(
        tile_index,
        step_offset,
        block_patch,
        ownership,
        from_low,
        from_high,
        interp_weight,
        own_panels,
    )
    got = lax.all_to_all(
        sent.reshape(devices, stride, points), ("bx", "by"), 0, 0, tiled=True
    ).reshape(devices * stride, points)

    pairs = near_pairs.shape[0]
    result = pl.pallas_call(
        functools.partial(near_kernel, comps=comps, slots=slots, stride=stride),
        out_shape=jax.ShapeDtypeStruct((owned * comps, points), f32),
        in_specs=[SMEM, VMEM, ANY],
        out_specs=VMEM,
        scratch_shapes=[
            pltpu.VMEM((owned * comps, points), f32),
            pltpu.VMEM((pairs, points, points), bf16),
            pltpu.SemaphoreType.DMA((pairs // PAIRS,)),
        ],
        compiler_params=kernel_params(32),
    )(near_pairs.reshape(-1), got, precorrection)
    return result.reshape(owned, comps, points)


def solution(mesh):
    placed = (
        P(None, "bx", "by", None),
        P(None, "bx", "by", None),
        P(("bx", "by"), None, None),
        P(("bx", "by")),
        P(("bx", "by")),
        P(("bx", "by")),
        P(),
        P(("bx", "by"), None),
        P(("bx", "by"), None, None),
    )
    return jax.shard_map(
        per_device,
        mesh=mesh,
        in_specs=placed,
        out_specs=P(("bx", "by"), None, None),
        check_vma=False,
    )
```

profile of v0, /device:TPU:0, one launch (start us, length us, event | category | flops | bytes accessed | tf_op | source)
XLA Modules:
  0.0 139.0 jit_solution(12650127676388339353)
XLA Ops:
  0.0 1.9 %fusion = (f32[4,16,4,256]{3,2,1,0:T(4,128)S(1)}, f32[4,16,4,256]{3,2,1,0:T(4,128)S(1)}, f32[4,16,4,256]{3,2,1,0:T(4,128)S(1)}, f32[4,16,4,256]{3,2,1,0:T(4,128)S(1)}) fusion(f32[4,16,32,256]{3,2,1,0:T(8,128)} %now.3, f32[4,16,32,256]{3,2,1,0:T(8,128)} %before.3), kind=kLoop, calls=%fused_computation.2 | loop fusion | bytes 2097152 | tf_op jit(solution)/shard_map/slice | solution.py:529
  1.9 0.1 pad_maximum_fusion
  2.0 2.4 %collective-permute-start = (f32[4,16,8,256]{3,2,1,0:T(8,128)S(1)}, f32[4,16,8,256]{3,2,1,0:T(8,128)S(1)}, u32[]{:S(2)}, u32[]{:S(2)}) collective-permute-start(f32[4,16,8,256]{3,2,1,0:T(8,128)S(1)} %pad_maximum_fusion), channel_id=1, source_target_pairs={{0,1},{1,2},{2,3},{3,4},{4,5},{5,6},{6,7},{8,9},{9,10},{10,11},{11... | collective-permute-start | bytes 1572872 | tf_op jit(solution)/shard_map/ppermute | solution.py:526
  4.4 0.1 pad_maximum_fusion.1
  4.6 0.0 copy-start.4
  4.6 0.0 copy-start.5
  4.6 1.3 collective-permute-start.1
  5.9 0.0 collective-permute-done.y_low
  5.9 4.5 %collective-permute-done.1.y_high = f32[4,16,8,256]{3,2,1,0:T(8,128)S(1)} collective-permute-done((f32[4,16,8,256]{3,2,1,0:T(8,128)S(1)}, f32[4,16,8,256]{3,2,1,0:T(8,128)S(1)}, u32[]{:S(2)}, u32[]{:S(2)}) %collective-permute-start.1) | collective-permute-done | bytes 524320 | tf_op jit(solution)/shard_map/ppermute | solution.py:526
  10.5 0.0 copy-done.1
  10.5 0.0 copy-done
  10.5 2.3 %shard_map.91 = (f32[4,2,144,128]{3,2,1,0:T(8,128)S(1)}, f32[4,2,144,128]{3,2,1,0:T(8,128)S(1)}) custom-call(f32[4,16,32,256]{3,2,1,0:T(8,128)S(1)} %copy-done, f32[4,16,32,256]{3,2,1,0:T(8,128)S(1)} %copy-done.1, f32[4,16,8,256]{3,2,1,0:T(8,128)S(1)} %collective-permute-done.y_low, f32[4,16,8,256]{3,2,1,0:T(8,128)S(1)} %collective-permute-done.1.y_high), custom_call_target="tpu_custom_call" | custom-call | tf_op jit(solution)/shard_map/pallas_call | solution.py:535
  12.7 3.5 %collective-permute-start.2 = (f32[4,2,144,128]{3,2,1,0:T(8,128)S(1)}, f32[4,2,144,128]{3,2,1,0:T(8,128)S(1)}, u32[]{:S(2)}, u32[]{:S(2)}) collective-permute-start(f32[4,2,144,128]{3,2,1,0:T(8,128)S(1)} %get-tuple-element.7), channel_id=1, source_target_pairs={{0,8},{8,16},{16,24},{1,9},{9,17},{17,25},{2,10},{10,18},{18,26},{... | collective-permute-start | bytes 1769480 | tf_op jit(solution)/shard_map/ppermute | solution.py:526
  16.3 0.0 copy-start.3
  16.3 0.0 copy-start.6
  16.3 1.3 collective-permute-start.3
  17.6 0.0 copy-done.4
  17.6 0.0 copy-done.5
  17.6 45.7 %shard_map.92.own_panels = f32[512,128]{1,0:T(8,128)S(1)} custom-call(s32[128]{0:T(128)S(1)} %copy-done.4, s32[128]{0:T(128)S(1)} %copy-done.5, f32[4,16,32,256]{3,2,1,0:T(8,128)} %now.3, f32[4,16,32,256]{3,2,1,0:T(8,128)} %before.3, f32[4,16,8,256]{3,2,1,0:T(8,128)S(1)} %collective-permute-done.y_low, f32[4,16,8,256]{3,2,1,0:T(8,128)S(1)} %collective-permute-done.1.y_high, ...), custom_call_target="tpu_custom_call" | custom-call | tf_op jit(solution)/shard_map/pallas_call | solution.py:547
  63.3 0.0 copy-start.7
  63.3 0.0 collective-permute-done.2.from_low
  63.3 0.0 collective-permute-done.3.from_high
  63.3 0.0 copy-done.3
  63.3 0.0 copy-done.6
  63.4 35.6 %shard_map.93 = f32[1280,128]{1,0:T(8,128)} custom-call(s32[128]{0:T(128)S(1)} %copy-done.4, s32[128]{0:T(128)S(1)} %copy-done.5, s32[128]{0:T(128)S(1)} %copy-done.6, s32[2048]{0:T(1024)S(1)} %copy-done.3, f32[4,2,144,128]{3,2,1,0:T(8,128)S(1)} %collective-permute-done.2.from_low, f32[4,2,144,128]{3,2,1,0:T(8,128)S(1)} %collective-permute-done.3.from_high, ...), custom_call_target="tpu_custom_call" | custom-call | tf_op jit(solution)/shard_map/pallas_call | solution.py:567
  98.9 14.9 %all-to-all-start = ((f32[32,40,128]{2,1,0:T(8,128)}), f32[32,40,128]{2,1,0:T(8,128)S(1)}, u32[]{:S(2)}, u32[]{:S(2)}) async-start(f32[32,40,128]{2,1,0:T(8,128)} %bitcast.4), calls=%async_computation | async-start | bytes 1310720 | tf_op jit(solution)/shard_map/all_to_all | solution.py:600
  113.9 0.0 copy-done.7
  113.9 0.1 copy.10
  114.0 0.1 reshape.12.pairs
  114.1 17.7 %all-to-all-done = f32[32,40,128]{2,1,0:T(8,128)S(1)} async-done(((f32[32,40,128]{2,1,0:T(8,128)}), f32[32,40,128]{2,1,0:T(8,128)S(1)}, u32[]{:S(2)}, u32[]{:S(2)}) %all-to-all-start) | async-done | bytes 655392 | tf_op jit(solution)/shard_map/all_to_all | solution.py:600
  131.8 2.2 %copy-done.2 = bf16[128,128,128]{2,1,0:T(8,128)(2,1)S(1)} copy-done((bf16[128,128,128]{2,1,0:T(8,128)(2,1)S(1)}, bf16[128,128,128]{2,1,0:T(8,128)(2,1)}, u32[]{:S(2)}) %copy-start.2) | copy-done | bytes 4194328
  134.0 5.0 %shard_map.94 = f32[256,128]{1,0:T(8,128)} custom-call(s32[256]{0:T(256)S(1)} %reshape.12.pairs, f32[1280,128]{1,0:T(8,128)S(1)} %bitcast.3, bf16[128,128,128]{2,1,0:T(8,128)(2,1)S(1)} %copy-done.2), custom_call_target="tpu_custom_call" | custom-call | tf_op jit(solution)/shard_map/pallas_call | solution.py:605
  (3 shorter events, 0.0 us)
Async XLA Ops:
  0.0 10.5 %copy-start.1 = (f32[4,16,32,256]{3,2,1,0:T(8,128)S(1)}, f32[4,16,32,256]{3,2,1,0:T(8,128)}, u32[]{:S(2)}) copy-start(f32[4,16,32,256]{3,2,1,0:T(8,128)} %before.3) | copy-start | bytes 6291460
  0.0 10.5 %copy-start = (f32[4,16,32,256]{3,2,1,0:T(8,128)S(1)}, f32[4,16,32,256]{3,2,1,0:T(8,128)}, u32[]{:S(2)}) copy-start(f32[4,16,32,256]{3,2,1,0:T(8,128)} %now.3) | copy-start | bytes 6291460
  2.0 3.9 %collective-permute-start = (f32[4,16,8,256]{3,2,1,0:T(8,128)S(1)}, f32[4,16,8,256]{3,2,1,0:T(8,128)S(1)}, u32[]{:S(2)}, u32[]{:S(2)}) collective-permute-start(f32[4,16,8,256]{3,2,1,0:T(8,128)S(1)} %pad_maximum_fusion), channel_id=1, source_target_pairs={{0,1},{1,2},{2,3},{3,4},{4,5},{5,6},{6,7},{8,9},{9,10},{10,11},{11... | collective-permute-start | bytes 1572872 | tf_op jit(solution)/shard_map/ppermute | solution.py:526
  4.6 13.0 %copy-start.4 = (s32[128]{0:T(128)S(1)}, s32[128]{0:T(128)}, u32[]{:S(2)}) copy-start(s32[128]{0:T(128)} %tile_index.3) | copy-start | bytes 1540
  4.6 13.0 %copy-start.5 = (s32[128]{0:T(128)S(1)}, s32[128]{0:T(128)}, u32[]{:S(2)}) copy-start(s32[128]{0:T(128)} %step_offset.3) | copy-start | bytes 1540
  4.6 5.9 %collective-permute-start.1 = (f32[4,16,8,256]{3,2,1,0:T(8,128)S(1)}, f32[4,16,8,256]{3,2,1,0:T(8,128)S(1)}, u32[]{:S(2)}, u32[]{:S(2)}) collective-permute-start(f32[4,16,8,256]{3,2,1,0:T(8,128)S(1)} %pad_maximum_fusion.1), channel_id=1, source_target_pairs={{1,0},{2,1},{3,2},{4,3},{5,4},{6,5},{7,6},{9,8},{10,9},{11,10},{12... | collective-permute-start | bytes 1572872 | tf_op jit(solution)/shard_map/ppermute | solution.py:526
  12.7 50.6 %collective-permute-start.2 = (f32[4,2,144,128]{3,2,1,0:T(8,128)S(1)}, f32[4,2,144,128]{3,2,1,0:T(8,128)S(1)}, u32[]{:S(2)}, u32[]{:S(2)}) collective-permute-start(f32[4,2,144,128]{3,2,1,0:T(8,128)S(1)} %get-tuple-element.7), channel_id=1, source_target_pairs={{0,8},{8,16},{16,24},{1,9},{9,17},{17,25},{2,10},{10,18},{18,26},{... | collective-permute-start | bytes 1769480 | tf_op jit(solution)/shard_map/ppermute | solution.py:526
  16.3 47.1 %copy-start.3 = (s32[2048]{0:T(1024)S(1)}, s32[2048]{0:T(1024)}, u32[]{:S(2)}) copy-start(s32[2048]{0:T(1024)} %ownership.1) | copy-start | bytes 24580
  16.3 47.1 %copy-start.6 = (s32[128]{0:T(128)S(1)}, s32[128]{0:T(128)}, u32[]{:S(2)}) copy-start(s32[128]{0:T(128)} %block_patch.1) | copy-start | bytes 1540
  16.3 47.0 %collective-permute-start.3 = (f32[4,2,144,128]{3,2,1,0:T(8,128)S(1)}, f32[4,2,144,128]{3,2,1,0:T(8,128)S(1)}, u32[]{:S(2)}, u32[]{:S(2)}) collective-permute-start(f32[4,2,144,128]{3,2,1,0:T(8,128)S(1)} %get-tuple-element.8), channel_id=1, source_target_pairs={{8,0},{16,8},{24,16},{9,1},{17,9},{25,17},{10,2},{18,10},{26,18},{... | collective-permute-start | bytes 1769480 | tf_op jit(solution)/shard_map/ppermute | solution.py:526
  63.3 50.6 %copy-start.7 = (s32[128,2]{0,1:T(2,128)S(1)}, s32[128,2]{0,1:T(2,128)}, u32[]{:S(2)}) copy-start(s32[128,2]{0,1:T(2,128)} %param.16) | copy-start | bytes 3076
  98.9 32.8 %all-to-all-start = ((f32[32,40,128]{2,1,0:T(8,128)}), f32[32,40,128]{2,1,0:T(8,128)S(1)}, u32[]{:S(2)}, u32[]{:S(2)}) async-start(f32[32,40,128]{2,1,0:T(8,128)} %bitcast.4), calls=%async_computation | async-start | bytes 1310720 | tf_op jit(solution)/shard_map/all_to_all | solution.py:600
  131.8 2.2 %copy-start.2 = (bf16[128,128,128]{2,1,0:T(8,128)(2,1)S(1)}, bf16[128,128,128]{2,1,0:T(8,128)(2,1)}, u32[]{:S(2)}) copy-start(bf16[128,128,128]{2,1,0:T(8,128)(2,1)} %precorrection.1) | copy-start | bytes 12582916
where the time goes:
time: 139 us
  Pallas kernels  88.5 us (64%)
  starting transfers between devices  23.4 us (17%)
  waiting for transfers between devices  22.2 us (16%)
  local copies, waits for them, and re-layouts  4.38 us (3%)
    pallas_call x1, Pallas kernels, per_device(): pl.pallas_call(own_kernel, out_shape=jax.ShapeDtypeStruct((blocks * comps...  45.7 us
    pallas_call x1, Pallas kernels, per_device(): pl.pallas_call(functools.partial(share_kernel, size_x=size_x, size_y=size...  35.6 us
    all_to_all x1, waiting for transfers between devices, per_device(): lax.all_to_all(sent.reshape(devices, stride, points), ('bx', 'by'), 0, 0,...  17.7 us
    all_to_all x1, starting transfers between devices, per_device(): lax.all_to_all(sent.reshape(devices, stride, points), ('bx', 'by'), 0, 0,...  14.9 us
    ppermute x4, starting transfers between devices, swap(): return (lax.ppermute(up, axis, forward), lax.ppermute(down, axis, backward))  8.49 us
    pallas_call x1, Pallas kernels, per_device(): pl.pallas_call(functools.partial(near_kernel, comps=comps, slots=slots, s...  4.98 us
    ppermute x4, waiting for transfers between devices, swap(): return (lax.ppermute(up, axis, forward), lax.ppermute(down, axis, backward))  4.58 us
  transfers between devices with their start and end apart: 5, of which 2 were waited for; matrix products, arithmetic and copies ran while one was open for 0% of the time, Pallas kernels for 33%

commit v1 on v0

v1 whole, which is shorter than its diff:
```python
import functools

import jax
import jax.numpy as jnp
from jax import lax
from jax.experimental import pallas as pl
from jax.experimental.pallas import tpu as pltpu
from jax.sharding import PartitionSpec as P

STEPS = 4
COEF = 0.3
LANES = 128
TILE = 8
OWN = 8
MEGA = 1 << 20


def ceil8(n):
    return (n + 7) // 8 * 8


def edge_rows():
    at_low = lax.axis_index("by") == 0
    at_high = lax.axis_index("by") == lax.axis_size("by") - 1
    row = lax.broadcasted_iota(jnp.int32, (8, LANES), 0)
    keep_low = row >= jnp.where(at_low, STEPS, 0)
    keep_high = row < jnp.where(at_high, 8 - STEPS, 8)
    return keep_low, keep_high


def beside_z(mid):
    halves = len(mid)
    lane = lax.broadcasted_iota(jnp.int32, mid[0].shape, 1)
    first = lane == 0
    last = lane == LANES - 1
    up = [pltpu.roll(m, 1, 1) for m in mid]
    down = [pltpu.roll(m, LANES - 1, 1) for m in mid]
    sums = []
    for h in range(halves):
        below = jnp.where(first, up[h - 1] if h else 0.0, up[h])
        above = jnp.where(last, down[h + 1] if h + 1 < halves else 0.0, down[h])
        sums.append(below + above)
    return sums


def load(ref, c, slot, start, rows):
    return [ref[h, c, slot, start : start + rows, :] for h in range(ref.shape[0])]


def advance(cur, old, c, slot, mid, beside, edges, keep=None):
    rows = mid[0].shape[0]
    start = OWN if edges is None else OWN - STEPS
    across = beside_z(mid)
    for h in range(len(mid)):
        total = across[h] + cur[h, c, slot, start - 1 : start - 1 + rows, :]
        total = total + cur[h, c, slot, start + 1 : start + 1 + rows, :]
        for plane in beside:
            total = total + plane[h]
        before = old[h, c, slot, start : start + rows, :]
        fresh = (2.0 - 6.0 * COEF) * mid[h] - before + COEF * total
        if keep is not None:
            fresh = jnp.where(keep, fresh, 0.0)
        if edges is None:
            old[h, c, slot, start : start + rows, :] = fresh
            continue
        old[h, c, slot, start : start + 8, :] = jnp.where(edges[0], fresh[:8], 0.0)
        old[h, c, slot, start + 8 : start + rows - 8, :] = fresh[8 : rows - 8]
        old[h, c, slot, start + rows - 8 : start + rows, :] = jnp.where(
            edges[1], fresh[rows - 8 :], 0.0
        )


def fill_rows(now, before, c, slot, y_low, y_high, x, size_y):
    for h in range(now.shape[0]):
        z = slice(h * LANES, (h + 1) * LANES)
        top = OWN + size_y
        now[h, c, slot, OWN - STEPS : OWN, :] = y_low[c, x, :STEPS, z]
        before[h, c, slot, OWN - STEPS : OWN, :] = y_low[c, x, STEPS:, z]
        now[h, c, slot, top : top + STEPS, :] = y_high[c, x, :STEPS, z]
        before[h, c, slot, top : top + STEPS, :] = y_high[c, x, STEPS:, z]


def faces_kernel(near_now, near_before, y_low, y_high, out_low, out_high, p_now, p_before):
    halves, comps, _, size_y, _ = near_now.shape
    size_x = y_low.shape[1]
    rows = size_y + 2 * STEPS
    near = STEPS

    def slot(face, depth):
        return depth + 2 if face == 0 else 9 - depth

    edges = edge_rows()
    outs = (out_low, out_high)

    def prepare(c, carry):
        for face in range(2):
            for depth in range(near):
                x = depth if face == 0 else size_x - 1 - depth
                place = depth if face == 0 else 2 * near - 1 - depth
                for h in range(halves):
                    own = slice(OWN, OWN + size_y)
                    p_now[h, c, slot(face, depth), own, :] = near_now[h, c, place]
                    p_before[h, c, slot(face, depth), own, :] = near_before[h, c, place]
                fill_rows(p_now, p_before, c, slot(face, depth), y_low, y_high, x, size_y)
            for depth in (-1, -2):
                for h in range(halves):
                    zero = jnp.zeros((rows + 8, LANES), jnp.float32)
                    p_now[h, c, slot(face, depth)] = zero
                    p_before[h, c, slot(face, depth)] = zero
        return carry

    lax.fori_loop(0, comps, prepare, 0)

    def give(buf, c, step, offset):
        more = STEPS - 1 - step
        for face in range(2):
            place = slot(face, 0)
            for h in range(halves):
                outs[face][c, h, step * size_y : (step + 1) * size_y, :] = buf[
                    h, c, place, OWN : OWN + size_y, :
                ]
                if more:
                    base = STEPS * size_y + offset
                    outs[face][c, h, base : base + more, :] = buf[h, c, place, OWN - more : OWN, :]
                    outs[face][c, h, base + more : base + 2 * more, :] = buf[
                        h, c, place, OWN + size_y : OWN + size_y + more, :
                    ]

    def evolve(c, carry):
        cur, old = p_now, p_before
        give(cur, c, 0, 0)
        offset = 2 * (STEPS - 1)
        for step, depths in ((1, (-1, 0, 1, 2)), (2, (-1, 0, 1)), (3, (0,))):
            for face in range(2):
                start = OWN - STEPS
                span = range(depths[0] - 1, depths[-1] + 2)
                mids = {d: load(cur, c, slot(face, d), start, rows) for d in span}
                for d in depths:
                    advance(cur, old, c, slot(face, d), mids[d], (mids[d - 1], mids[d + 1]), edges)
            cur, old = old, cur
            give(cur, c, step, offset)
            offset += 2 * (STEPS - 1 - step)
        for face in range(2):
            for h in range(halves):
                base = STEPS * size_y + offset
                outs[face][c, h, base : base + 4, :] = jnp.zeros((4, LANES), jnp.float32)
        return carry

    lax.fori_loop(0, comps, evolve, 0)


def identity(n, dtype):
    row = lax.broadcasted_iota(jnp.int32, (n, n), 0)
    col = lax.broadcasted_iota(jnp.int32, (n, n), 1)
    return (row == col).astype(jnp.float32).astype(dtype)


def turn_tile(read, eye):
    parts = []
    for h in range(eye.shape[0] // LANES):
        cells = read(h)
        parts.append(cells.reshape(-1, LANES).astype(jnp.bfloat16))
    cells = jnp.concatenate(parts, axis=1)
    return lax.dot_general(
        eye, cells, (((1,), (1,)), ((), ())), preferred_element_type=jnp.float32
    )


def fill_spread(spread, comps):
    rows, cols = spread.shape
    per = cols // comps
    part = rows // 2 // comps
    for c in range(comps):
        row = lax.broadcasted_iota(jnp.int32, (rows, per), 0)
        col = lax.broadcasted_iota(jnp.int32, (rows, per), 1) // TILE
        goal = col // part * (rows // 2) + c * part + col % part
        hot = row == goal
        spread[:, c * per : (c + 1) * per] = hot.astype(jnp.float32).astype(jnp.bfloat16)


def spread_tiles(cells_of, spread, lhs, first, comps, group):
    cells = jnp.concatenate([cells_of(first + b) for b in range(group)], axis=0)
    cells = cells.astype(jnp.bfloat16)
    per = lhs.shape[2]
    row = lax.broadcasted_iota(jnp.int32, (TILE, per), 0)
    col = lax.broadcasted_iota(jnp.int32, (TILE, per), 1) % TILE
    keep = row == col
    for pair in range(comps // 2):
        wide = [
            jnp.dot(
                cells, spread[:, c * per : (c + 1) * per], preferred_element_type=jnp.float32
            )
            for c in (2 * pair, 2 * pair + 1)
        ]
        for b in range(group):
            both = [jnp.where(keep, w[b * TILE : (b + 1) * TILE], 0.0) for w in wide]
            lhs[first + b, pair * 2 * TILE : (pair + 1) * 2 * TILE, :] = jnp.concatenate(
                both, axis=0
            ).astype(jnp.bfloat16)


SPREAD = 32
GROUP = 8


def panel_rows(lhs, weights, comps):
    panels = []
    height = comps * TILE
    for b in range(0, len(lhs), 2):
        left = jnp.concatenate([lhs[b], lhs[b + 1]], axis=0)
        right = jnp.concatenate([weights[b], weights[b + 1]], axis=1)
        made = jnp.dot(left, right, preferred_element_type=jnp.float32)
        half = made.shape[1] // 2
        for n, m in ((0, made[:height, :half]), (1, made[height:, half:])):
            panels.append(
                [
                    jnp.sum(m[c * TILE : (c + 1) * TILE], axis=0, keepdims=True)
                    for c in range(comps)
                ]
            )
    return panels


def place_kernel(
    block_patch, ownership, now, before, out, place, near_now, near_before, count, sems,
    *, slots, stride,
):
    comps, size_x, _, size_z = now.shape
    copies = []
    for a, (src, dst) in enumerate(((now, near_now), (before, near_before))):
        for face in range(2):
            x0 = 0 if face == 0 else size_x - STEPS
            for h in range(size_z // LANES):
                copies.append(
                    pltpu.make_async_copy(
                        src.at[:, x0 : x0 + STEPS, :, h * LANES : (h + 1) * LANES],
                        dst.at[h, :, face * STEPS : (face + 1) * STEPS],
                        sems.at[a, face, h],
                    )
                )
    for copy in copies:
        copy.start()
    blocks = block_patch.shape[0]
    devices = lax.axis_size("bx") * lax.axis_size("by")
    owned = ownership.shape[0] // devices
    out[...] = jnp.full(out.shape, -1.0, jnp.float32)

    def clear(d, carry):
        count[d] = 0
        return carry

    lax.fori_loop(0, devices, clear, 0, unroll=8)

    def one(b, carry):
        target = ownership[block_patch[b]]
        owner = target // owned
        rank = count[owner]
        count[owner] = rank + 1
        row = owner * stride + rank
        place[b] = row
        local = (target - owner * owned).astype(jnp.float32)
        out[pl.ds(row + comps * slots, 1), :] = jnp.full((1, LANES), local, jnp.float32)
        return carry

    lax.fori_loop(0, blocks, one, 0, unroll=8)
    for copy in copies:
        copy.wait()


def own_kernel(now, before, y_low, y_high, far, near, p_now, p_before, sems):
    comps, size_x, size_y, size_z = now.shape
    halves = size_z // LANES
    rows = size_y + 2 * STEPS
    tiles_y = size_y // TILE
    tiles_z = size_z // TILE
    columns = size_x // TILE * tiles_y
    copies = []
    for a, (src, dst) in enumerate(((now, p_now), (before, p_before))):
        for h in range(halves):
            copies.append(
                pltpu.make_async_copy(
                    src.at[:, :, :, h * LANES : (h + 1) * LANES],
                    dst.at[h, :, 2 : 2 + size_x, OWN : OWN + size_y, :],
                    sems.at[a, h],
                )
            )
    for copy in copies:
        copy.start()
    edges = edge_rows()
    keep_low = lax.axis_index("bx") > 0
    keep_high = lax.axis_index("bx") < lax.axis_size("bx") - 1

    def prepare(c, carry):
        def one(x, carry):
            fill_rows(p_now, p_before, c, x + 2, y_low, y_high, x, size_y)
            return carry

        lax.fori_loop(0, size_x, one, 0)
        for place in (0, 1, size_x + 2, size_x + 3):
            for h in range(halves):
                zero = jnp.zeros((rows + 8, LANES), jnp.float32)
                p_now[h, c, place] = zero
                p_before[h, c, place] = zero
        return carry

    lax.fori_loop(0, comps, prepare, 0)
    eye = identity(size_z, jnp.bfloat16)
    for copy in copies:
        copy.wait()
    cur, old = p_now, p_before
    for step in range(STEPS):
        out_planes = (1, 2, 1, 0)[step]

        def evolve(c, carry, cur=cur, old=old, out_planes=out_planes, step=step):
            last = step == STEPS - 1
            bounds = None if last else edges
            start, count = (OWN, size_y) if last else (OWN - STEPS, rows)
            first, end = -out_planes, size_x + out_planes
            mids = {}

            def plane(x):
                if x not in mids and -2 <= x < size_x + 2:
                    mids[x] = load(cur, c, x + 2, start, count)
                return mids.get(x)

            for x in range(first, end):
                beside = [p for p in (plane(x - 1), plane(x + 1)) if p is not None]
                keep = keep_low if x < 0 else keep_high if x >= size_x else None
                advance(cur, old, c, x + 2, plane(x), beside, bounds, keep)
                mids.pop(x - 1, None)
            return carry

        lax.fori_loop(0, comps, evolve, 0)

        for column in range(columns):
            face = column // tiles_y
            x0 = 2 + (STEPS if face == 0 else size_x - 2 * STEPS)
            y0 = OWN + column % tiles_y * TILE
            turned = turn_tile(lambda h: old[h, :, x0 : x0 + STEPS, y0 : y0 + TILE, :], eye)
            first = (step * columns + column) * tiles_z
            far[pl.ds(first, tiles_z)] = turned.reshape(tiles_z, TILE, comps * STEPS * TILE)
        for face in range(2):
            x0 = 2 + (0 if face == 0 else size_x - STEPS)
            for h in range(halves):
                near[step, h, :, face * STEPS : (face + 1) * STEPS] = old[
                    h, :, x0 : x0 + STEPS, OWN : OWN + size_y, :
                ]
        cur, old = old, cur


def share_kernel(
    tile_index, step_offset, place, base, from_low, from_high, far, near, weight, out,
    bound, d_now, d_before, table, held, spread, lhs, wsems, *, slots,
):
    _, halves, comps, _, size_y, _ = near.shape
    size_z = halves * LANES
    rows = size_y + 2 * STEPS
    blocks = weight.shape[0]
    tiles_y = size_y // TILE
    tiles_z = size_z // TILE
    columns = 2 * tiles_y

    def weights(g):
        part = pl.ds(g * GROUP, GROUP)
        return pltpu.make_async_copy(weight.at[part], held.at[part], wsems.at[g])

    for g in range(blocks // GROUP):
        weights(g).start()
    out[...] = base[...]
    edges = edge_rows()
    froms = (from_low, from_high)

    def prepare(c, carry):
        for face in range(2):
            offset = STEPS * size_y
            for step in range(STEPS):
                place = face * STEPS + step
                more = STEPS - 1 - step
                for h in range(halves):
                    src = froms[face]
                    bound[h, c, place, OWN : OWN + size_y, :] = src[
                        c, h, step * size_y : (step + 1) * size_y, :
                    ]
                    if more:
                        bound[h, c, place, OWN - more : OWN, :] = src[
                            c, h, offset : offset + more, :
                        ]
                        bound[h, c, place, OWN + size_y : OWN + size_y + more, :] = src[
                            c, h, offset + more : offset + 2 * more, :
                        ]
                offset += 2 * more
            for place in range(face * STEPS, (face + 1) * STEPS):
                for h in range(halves):
                    zero = jnp.zeros((rows + 8, LANES), jnp.float32)
                    d_now[h, c, place] = zero
                    d_before[h, c, place] = zero
        return carry

    lax.fori_loop(0, comps, prepare, 0)
    fill_spread(spread, comps)
    eye = identity(size_z, jnp.bfloat16)

    def slot(face, depth):
        return depth if face == 0 else 2 * STEPS - 1 - depth

    cur, old = d_now, d_before
    for step in range(STEPS):

        def evolve(c, carry, cur=cur, old=old, step=step):
            last = step == STEPS - 1
            bounds = None if last else edges
            start, count = (OWN, size_y) if last else (OWN - STEPS, rows)
            for face in range(2):
                mids = {
                    d: load(cur, c, slot(face, d), start, count)
                    for d in range(min(step + 2, STEPS))
                }
                mids[-1] = load(bound, c, face * STEPS + step, start, count)
                for d in range(step + 1):
                    beside = [mids[x] for x in (d - 1, d + 1) if x in mids]
                    advance(cur, old, c, slot(face, d), mids[d], beside, bounds)
            return carry

        for c in range(comps):
            evolve(c, 0)

        for column in range(columns):
            x0 = column // tiles_y * STEPS
            y0 = column % tiles_y * TILE

            def read(h):
                kept = near[step, h, :, x0 : x0 + STEPS, y0 : y0 + TILE, :]
                return kept + old[h, :, x0 : x0 + STEPS, OWN + y0 : OWN + y0 + TILE, :]

            turned = turn_tile(read, eye)
            first = (step * columns + column) * tiles_z
            table[pl.ds(first, tiles_z)] = turned.reshape(tiles_z, TILE, comps * STEPS * TILE)
        cur, old = old, cur

    def panels(g, carry):
        weights(g).wait()
        made = panel_rows(
            [lhs[g * GROUP + b] for b in range(GROUP)],
            [held[g * GROUP + b] for b in range(GROUP)],
            comps,
        )
        for b in range(GROUP):
            row = place[g * GROUP + b]
            for c in range(comps):
                out[pl.ds(row + c * slots, 1), :] = made[b][c]
        return carry

    def cells_of(block):
        tile = tile_index[block]
        at = step_offset[block] * (columns * tiles_z) + tile
        low = tile < tiles_y * tiles_z
        a, b = table[at], far[at]
        return jnp.concatenate([jnp.where(low, a, b), jnp.where(low, b, a)], axis=1)

    def widen(g, carry):
        spread_tiles(cells_of, spread, lhs, g * SPREAD, comps, SPREAD)
        return carry

    lax.fori_loop(0, blocks // SPREAD, widen, 0)
    lax.fori_loop(0, blocks // GROUP, panels, 0)


PAIRS = 16


def near_kernel(pairs, got, precorrection, out, field, total, held, sems, *, comps, slots, stride):
    count = precorrection.shape[0]
    senders = got.shape[0] // stride
    owned = out.shape[0] // comps

    def blocks(g):
        part = pl.ds(g * PAIRS, PAIRS)
        return pltpu.make_async_copy(precorrection.at[part], held.at[part], sems.at[g])

    for g in range(count // PAIRS):
        blocks(g).start()
    field[...] = jnp.zeros(field.shape, jnp.float32)
    whole = got[...].reshape(senders, stride, LANES)
    ids = whole[:, comps * slots : (comps + 1) * slots, :].reshape(senders * slots, LANES)
    ids = ids.T[:owned]
    hot = ids == lax.broadcasted_iota(jnp.int32, ids.shape, 0).astype(jnp.float32)
    hot = hot.astype(jnp.float32).astype(jnp.bfloat16)
    for c in range(comps):
        rest = whole[:, c * slots : (c + 1) * slots, :].reshape(senders * slots, LANES)
        summed = None
        for _ in range(3):
            piece = rest.astype(jnp.bfloat16)
            rest = rest - piece.astype(jnp.float32)
            part = jnp.dot(hot, piece, preferred_element_type=jnp.float32)
            summed = part if summed is None else summed + part
        field[pl.ds(c, owned, stride=TILE), :] = summed
    total[...] = field[...]
    empty = jnp.zeros((TILE, LANES), jnp.float32)

    def group(g, carry):
        blocks(g).wait()
        made = []
        for b in range(0, PAIRS, 4):
            k = g * PAIRS + b
            rows = []
            for n in range(4):
                source = field[pl.ds(pl.multiple_of(pairs[2 * (k + n) + 1] * TILE, TILE), TILE), :]
                both = [source, empty] if n % 2 == 0 else [empty, source]
                rows.append(jnp.concatenate(both, axis=1))
            left = jnp.concatenate(rows, axis=0).astype(jnp.bfloat16)
            right = jnp.concatenate(
                [
                    jnp.concatenate([held[k], held[k + 2]], axis=1),
                    jnp.concatenate([held[k + 1], held[k + 3]], axis=1),
                ],
                axis=0,
            )
            four = jnp.dot(left, right, preferred_element_type=jnp.float32)
            for n in range(4):
                lane = n // 2 * LANES
                made.append(four[n * TILE : (n + 1) * TILE, lane : lane + LANES])
        for b in range(PAIRS):
            at = pl.ds(pl.multiple_of(pairs[2 * (g * PAIRS + b)] * TILE, TILE), TILE)
            total[at, :] += made[b]
        return carry

    lax.fori_loop(0, count // PAIRS, group, 0)
    for c in range(comps):
        out[pl.ds(c, owned, stride=comps), :] = total[pl.ds(c, owned, stride=TILE), :]


SMEM = pl.BlockSpec(memory_space=pltpu.SMEM)
VMEM = pl.BlockSpec(memory_space=pltpu.VMEM)
HBM = pl.BlockSpec(memory_space=pltpu.HBM)


def in_hbm(a):
    return pltpu.with_memory_space_constraint(a, pltpu.HBM)


def kernel_params(mib):
    return pltpu.CompilerParams(vmem_limit_bytes=mib * MEGA)


def per_device(
    field_now,
    field_before,
    interp_weight,
    tile_index,
    step_offset,
    block_patch,
    ownership,
    near_pairs,
    precorrection,
):
    comps, size_x, size_y, size_z = field_now.shape
    count_x = lax.axis_size("bx")
    count_y = lax.axis_size("by")
    devices = count_x * count_y
    blocks, cells, points = interp_weight.shape
    capacity = max(2, (2 * blocks + devices - 1) // devices)
    owned = ownership.shape[0] // devices
    halves = size_z // LANES
    rows = size_y + 2 * OWN
    f32, bf16 = jnp.float32, jnp.bfloat16

    def swap(up, down, axis, count):
        forward = [(i, i + 1) for i in range(count - 1)]
        backward = [(b, a) for a, b in forward]
        return lax.ppermute(up, axis, forward), lax.ppermute(down, axis, backward)

    slots = ceil8(capacity)
    stride = (comps + 1) * slots
    sent_shape = jax.ShapeDtypeStruct((devices * stride, points), f32)

    last, first = slice(size_y - STEPS, size_y), slice(0, STEPS)
    up = jnp.concatenate([field_now[:, :, last], field_before[:, :, last]], axis=2)
    down = jnp.concatenate([field_now[:, :, first], field_before[:, :, first]], axis=2)
    y_low, y_high = swap(up, down, "by", count_y)

    near_shape = jax.ShapeDtypeStruct((halves, comps, 2 * STEPS, size_y, LANES), f32)
    base, place, near_now, near_before = pl.pallas_call(
        functools.partial(place_kernel, slots=slots, stride=stride),
        out_shape=(
            sent_shape, jax.ShapeDtypeStruct((blocks,), jnp.int32), near_shape, near_shape
        ),
        in_specs=[SMEM, SMEM, HBM, HBM],
        out_specs=(VMEM, SMEM, VMEM, VMEM),
        scratch_shapes=[
            pltpu.SMEM((devices,), jnp.int32), pltpu.SemaphoreType.DMA((2, 2, halves))
        ],
    )(block_patch, ownership, in_hbm(field_now), in_hbm(field_before))

    face_rows = STEPS * size_y + ceil8(STEPS * (STEPS - 1) + 4)
    face = jax.ShapeDtypeStruct((comps, halves, face_rows, LANES), f32)
    plane = pltpu.VMEM((halves, comps, 12, rows, LANES), f32)
    give_low, give_high = pl.pallas_call(
        faces_kernel,
        out_shape=(face, face),
        in_specs=[VMEM, VMEM, VMEM, VMEM],
        out_specs=(VMEM, VMEM),
        scratch_shapes=[plane, plane],
        compiler_params=kernel_params(24),
    )(near_now, near_before, y_low, y_high)
    from_low, from_high = swap(give_high, give_low, "bx", count_x)

    tiles = size_x // TILE * (size_y // TILE) * (size_z // TILE)
    brick = pltpu.VMEM((halves, comps, size_x + 4, rows, LANES), f32)
    half = comps * STEPS * TILE
    far, near = pl.pallas_call(
        own_kernel,
        out_shape=(
            jax.ShapeDtypeStruct((STEPS * tiles, TILE, half), f32),
            jax.ShapeDtypeStruct((STEPS,) + near_shape.shape, f32),
        ),
        in_specs=[HBM, HBM, VMEM, VMEM],
        out_specs=(VMEM, VMEM),
        scratch_shapes=[brick, brick, pltpu.SemaphoreType.DMA((2, halves))],
        compiler_params=kernel_params(24),
    )(in_hbm(field_now), in_hbm(field_before), y_low, y_high)

    thin = pltpu.VMEM((halves, comps, 2 * STEPS, rows, LANES), f32)
    sent = pl.pallas_call(
        functools.partial(share_kernel, slots=slots),
        out_shape=sent_shape,
        in_specs=[SMEM, SMEM, SMEM, VMEM, VMEM, VMEM, VMEM, VMEM, HBM],
        out_specs=VMEM,
        scratch_shapes=[
            thin,
            thin,
            thin,
            pltpu.VMEM((STEPS * tiles, TILE, half), f32),
            pltpu.VMEM((blocks, cells, points), bf16),
            pltpu.VMEM((2 * half, comps * cells), bf16),
            pltpu.VMEM((blocks, comps * TILE, cells), bf16),
            pltpu.SemaphoreType.DMA((blocks // GROUP,)),
        ],
        compiler_params=kernel_params(40),
    )(
        tile_index, step_offset, place, base, from_low, from_high, far, near,
        in_hbm(interp_weight),
    )
    got = lax.all_to_all(
        sent.reshape(devices, stride, points), ("bx", "by"), 0, 0, tiled=True
    ).reshape(devices * stride, points)

    pairs = near_pairs.shape[0]
    result = pl.pallas_call(
        functools.partial(near_kernel, comps=comps, slots=slots, stride=stride),
        out_shape=jax.ShapeDtypeStruct((owned * comps, points), f32),
        in_specs=[SMEM, VMEM, HBM],
        out_specs=VMEM,
        scratch_shapes=[
            pltpu.VMEM((owned * TILE, points), f32),
            pltpu.VMEM((owned * TILE, points), f32),
            pltpu.VMEM((pairs, points, points), bf16),
            pltpu.SemaphoreType.DMA((pairs // PAIRS,)),
        ],
        compiler_params=kernel_params(32),
    )(near_pairs.reshape(-1), got, in_hbm(precorrection))
    return result.reshape(owned, comps, points)


def solution(mesh):
    placed = (
        P(None, "bx", "by", None),
        P(None, "bx", "by", None),
        P(("bx", "by"), None, None),
        P(("bx", "by")),
        P(("bx", "by")),
        P(("bx", "by")),
        P(),
        P(("bx", "by"), None),
        P(("bx", "by"), None, None),
    )
    return jax.shard_map(
        per_device,
        mesh=mesh,
        in_specs=placed,
        out_specs=P(("bx", "by"), None, None),
        check_vma=False,
    )
```

time: 139 us -> 82.3 us (0.59)
  Pallas kernels: 88.5 us -> 33 us
  waiting for transfers between devices: 22.2 us -> 18.2 us
  starting transfers between devices: 23.4 us -> 25.7 us
    pallas_call x3 -> x4, Pallas kernels: 83.5 us -> 28.7 us  [the longest x1 11.4 us: per_device(): pl.pallas_call(functools.partial(share_kernel, slots=slots), out_shape=se...]
    ppermute x4, waiting for transfers between devices: 4.58 us -> 0.58 us  [swap(): return (lax.ppermute(up, axis, forward), lax.ppermute(down, axis, backward))]
    all_to_all x1, starting transfers between devices: 14.9 us -> 17 us  [per_device(): lax.all_to_all(sent.reshape(devices, stride, points), ('bx', 'by'), 0, 0,...]
  transfers between devices with their start and end apart: 5 -> 5, of which waited for: 2 -> 2; matrix products, arithmetic and copies ran while one was open for 0% -> 0% of each run, Pallas kernels for 33% -> 18%
where the time goes in v1:
time: 82.3 us; the launch traced here: 81.8 us
  Pallas kernels  33 us (40%)
  starting transfers between devices  25.7 us (31%)
  waiting for transfers between devices  18.2 us (22%)
  local copies, waits for them, and re-layouts  4.48 us (5%)
    all_to_all x1, waiting for transfers between devices, per_device(): lax.all_to_all(sent.reshape(devices, stride, points), ('bx', 'by'), 0, 0,...  17.7 us
    all_to_all x1, starting transfers between devices, per_device(): lax.all_to_all(sent.reshape(devices, stride, points), ('bx', 'by'), 0, 0,...  17 us
    pallas_call x1, Pallas kernels, per_device(): pl.pallas_call(functools.partial(share_kernel, slots=slots), out_shape=se...  11.4 us
    pallas_call x1, Pallas kernels, per_device(): pl.pallas_call(own_kernel, out_shape=(jax.ShapeDtypeStruct((STEPS * tiles...  11.1 us
    ppermute x4, starting transfers between devices, swap(): return (lax.ppermute(up, axis, forward), lax.ppermute(down, axis, backward))  8.76 us
    pallas_call x1, Pallas kernels, per_device(): pl.pallas_call(functools.partial(near_kernel, comps=comps, slots=slots, s...  4.26 us
    pallas_call x1, Pallas kernels, per_device(): pl.pallas_call(functools.partial(place_kernel, slots=slots, stride=stride...  3.98 us
    unnamed x15, local copies, waits for them, and re-layouts  2.58 us
  transfers between devices with their start and end apart: 5, of which 2 were waited for; matrix products, arithmetic and copies ran while one was open for 0% of the time, Pallas kernels for 18%

profile of v1, /device:TPU:0, one launch (start us, length us, event | category | flops | bytes accessed | tf_op | source)
XLA Modules:
  0.0 81.8 jit_solution(16357281826583373091)
XLA Ops:
  0.0 1.8 %fusion = (f32[4,16,4,256]{3,2,1,0:T(4,128)S(1)}, f32[4,16,4,256]{3,2,1,0:T(4,128)S(1)}, f32[4,16,4,256]{3,2,1,0:T(4,128)S(1)}, f32[4,16,4,256]{3,2,1,0:T(4,128)S(1)}) fusion(f32[4,16,32,256]{3,2,1,0:T(8,128)} %now.3, f32[4,16,32,256]{3,2,1,0:T(8,128)} %before.3), kind=kLoop, calls=%fused_computation.2 | loop fusion | bytes 2097152 | tf_op jit(solution)/shard_map/slice | solution.py:578
  1.8 0.1 pad_maximum_fusion
  1.9 2.4 %collective-permute-start = (f32[4,16,8,256]{3,2,1,0:T(8,128)S(1)}, f32[4,16,8,256]{3,2,1,0:T(8,128)S(1)}, u32[]{:S(2)}, u32[]{:S(2)}) collective-permute-start(f32[4,16,8,256]{3,2,1,0:T(8,128)S(1)} %pad_maximum_fusion), channel_id=1, source_target_pairs={{0,1},{1,2},{2,3},{3,4},{4,5},{5,6},{6,7},{8,9},{9,10},{10,11},{11... | collective-permute-start | bytes 1572872 | tf_op jit(solution)/shard_map/ppermute | solution.py:570
  4.3 0.1 pad_maximum_fusion.1
  4.4 1.3 %collective-permute-start.1 = (f32[4,16,8,256]{3,2,1,0:T(8,128)S(1)}, f32[4,16,8,256]{3,2,1,0:T(8,128)S(1)}, u32[]{:S(2)}, u32[]{:S(2)}) collective-permute-start(f32[4,16,8,256]{3,2,1,0:T(8,128)S(1)} %pad_maximum_fusion.1), channel_id=1, source_target_pairs={{1,0},{2,1},{3,2},{4,3},{5,4},{6,5},{7,6},{9,8},{10,9},{11,10},{12... | collective-permute-start | bytes 1572872 | tf_op jit(solution)/shard_map/ppermute | solution.py:570
  5.7 4.0 %shard_map.91 = (f32[1280,128]{1,0:T(8,128)}, s32[128]{0:T(128)}, f32[2,4,8,32,128]{4,3,2,1,0:T(8,128)}, f32[2,4,8,32,128]{4,3,2,1,0:T(8,128)}) custom-call(s32[128]{0:T(128)} %block_patch.1, s32[2048]{0:T(1024)} %ownership.1, f32[4,16,32,256]{3,2,1,0:T(8,128)} %now.3, f32[4,16,32,256]{3,2,1,0:T(8,128)} %before.3), custom_call_target="tpu_custom_call" | custom-call | tf_op jit(solution)/shard_map/pallas_call | solution.py:582
  9.7 0.0 collective-permute-done.y_low
  9.7 0.6 collective-permute-done.1.y_high
  10.3 0.0 copy-start
  10.3 1.2 %copy-done = f32[2,4,8,32,128]{4,3,2,1,0:T(8,128)S(1)} copy-done((f32[2,4,8,32,128]{4,3,2,1,0:T(8,128)S(1)}, f32[2,4,8,32,128]{4,3,2,1,0:T(8,128)}, u32[]{:S(2)}) %copy-start) | copy-done | bytes 1048600
  11.5 0.0 copy-start.1
  11.5 1.2 %copy-done.1 = f32[2,4,8,32,128]{4,3,2,1,0:T(8,128)S(1)} copy-done((f32[2,4,8,32,128]{4,3,2,1,0:T(8,128)S(1)}, f32[2,4,8,32,128]{4,3,2,1,0:T(8,128)}, u32[]{:S(2)}) %copy-start.1) | copy-done | bytes 1048600
  12.7 0.0 copy-start.2
  12.7 0.0 copy-start.3
  12.7 2.2 %shard_map.92 = (f32[4,2,144,128]{3,2,1,0:T(8,128)S(1)}, f32[4,2,144,128]{3,2,1,0:T(8,128)S(1)}) custom-call(f32[2,4,8,32,128]{4,3,2,1,0:T(8,128)S(1)} %copy-done, f32[2,4,8,32,128]{4,3,2,1,0:T(8,128)S(1)} %copy-done.1, f32[4,16,8,256]{3,2,1,0:T(8,128)S(1)} %collective-permute-done.y_low, f32[4,16,8,256]{3,2,1,0:T(8,128)S(1)} %collective-permute-done.1.y_high), custom_call_target="tpu_custom_call" | custom-call | tf_op jit(solution)/shard_map/pallas_call | solution.py:597
  14.9 3.8 %collective-permute-start.2 = (f32[4,2,144,128]{3,2,1,0:T(8,128)S(1)}, f32[4,2,144,128]{3,2,1,0:T(8,128)S(1)}, u32[]{:S(2)}, u32[]{:S(2)}) collective-permute-start(f32[4,2,144,128]{3,2,1,0:T(8,128)S(1)} %get-tuple-element.17), channel_id=1, source_target_pairs={{0,8},{8,16},{16,24},{1,9},{9,17},{17,25},{2,10},{10,18},{18,26},{... | collective-permute-start | bytes 1769480 | tf_op jit(solution)/shard_map/ppermute | solution.py:570
  18.7 1.3 %collective-permute-start.3 = (f32[4,2,144,128]{3,2,1,0:T(8,128)S(1)}, f32[4,2,144,128]{3,2,1,0:T(8,128)S(1)}, u32[]{:S(2)}, u32[]{:S(2)}) collective-permute-start(f32[4,2,144,128]{3,2,1,0:T(8,128)S(1)} %get-tuple-element.18), channel_id=1, source_target_pairs={{8,0},{16,8},{24,16},{9,1},{17,9},{25,17},{10,2},{18,10},{26,18},{... | collective-permute-start | bytes 1769480 | tf_op jit(solution)/shard_map/ppermute | solution.py:570
  20.0 11.1 %shard_map.93 = (f32[1024,8,128]{2,1,0:T(8,128)S(1)}, f32[4,2,4,8,32,128]{5,4,3,2,1,0:T(8,128)S(1)}) custom-call(f32[4,16,32,256]{3,2,1,0:T(8,128)} %now.3, f32[4,16,32,256]{3,2,1,0:T(8,128)} %before.3, f32[4,16,8,256]{3,2,1,0:T(8,128)S(1)} %collective-permute-done.y_low, f32[4,16,8,256]{3,2,1,0:T(8,128)S(1)} %collective-permute-done.1.y_high), custom_call_target="tpu_custom_call" | custom-call | tf_op jit(solution)/shard_map/pallas_call | solution.py:610
  31.1 0.0 collective-permute-done.2.from_low
  31.1 0.0 collective-permute-done.3.from_high
  31.2 0.0 copy-done.2
  31.2 0.0 copy-done.3
  31.2 0.0 copy-done.4
  31.2 0.0 copy-done.5
  31.2 0.0 copy-start.6
  31.2 11.4 %shard_map.94 = f32[1280,128]{1,0:T(8,128)} custom-call(s32[128]{0:T(128)S(1)} %copy-done.3, s32[128]{0:T(128)S(1)} %copy-done.4, s32[128]{0:T(128)S(1)} %copy-done.5, f32[1280,128]{1,0:T(8,128)S(1)} %copy-done.2, f32[4,2,144,128]{3,2,1,0:T(8,128)S(1)} %collective-permute-done.2.from_low, f32[4,2,144,128]{3,2,1,0:T(8,128)S(1)} %collective-permute-done.3.from_high, ...), custom_call_target="tpu_custom_call" | custom-call | tf_op jit(solution)/shard_map/pallas_call | solution.py:623
  42.7 17.0 %all-to-all-start = ((f32[32,40,128]{2,1,0:T(8,128)}), f32[32,40,128]{2,1,0:T(8,128)S(1)}, u32[]{:S(2)}, u32[]{:S(2)}) async-start(f32[32,40,128]{2,1,0:T(8,128)} %bitcast), calls=%async_computation | async-start | bytes 1310720 | tf_op jit(solution)/shard_map/all_to_all | solution.py:643
  59.7 0.0 copy-done.6
  59.7 0.1 copy.10
  59.8 0.1 reshape.12.pairs
  59.9 17.7 %all-to-all-done = f32[32,40,128]{2,1,0:T(8,128)S(1)} async-done(((f32[32,40,128]{2,1,0:T(8,128)}), f32[32,40,128]{2,1,0:T(8,128)S(1)}, u32[]{:S(2)}, u32[]{:S(2)}) %all-to-all-start) | async-done | bytes 655392 | tf_op jit(solution)/shard_map/all_to_all | solution.py:643
  77.6 4.3 %shard_map.95 = f32[256,128]{1,0:T(8,128)} custom-call(s32[256]{0:T(256)S(1)} %reshape.12.pairs, f32[1280,128]{1,0:T(8,128)S(1)} %bitcast.3, bf16[128,128,128]{2,1,0:T(8,128)(2,1)} %precorrection.1), custom_call_target="tpu_custom_call" | custom-call | tf_op jit(solution)/shard_map/pallas_call | solution.py:648
  (2 shorter events, 0.0 us)
Async XLA Ops:
  1.9 7.8 %collective-permute-start = (f32[4,16,8,256]{3,2,1,0:T(8,128)S(1)}, f32[4,16,8,256]{3,2,1,0:T(8,128)S(1)}, u32[]{:S(2)}, u32[]{:S(2)}) collective-permute-start(f32[4,16,8,256]{3,2,1,0:T(8,128)S(1)} %pad_maximum_fusion), channel_id=1, source_target_pairs={{0,1},{1,2},{2,3},{3,4},{4,5},{5,6},{6,7},{8,9},{9,10},{10,11},{11... | collective-permute-start | bytes 1572872 | tf_op jit(solution)/shard_map/ppermute | solution.py:570
  4.4 5.9 %collective-permute-start.1 = (f32[4,16,8,256]{3,2,1,0:T(8,128)S(1)}, f32[4,16,8,256]{3,2,1,0:T(8,128)S(1)}, u32[]{:S(2)}, u32[]{:S(2)}) collective-permute-start(f32[4,16,8,256]{3,2,1,0:T(8,128)S(1)} %pad_maximum_fusion.1), channel_id=1, source_target_pairs={{1,0},{2,1},{3,2},{4,3},{5,4},{6,5},{7,6},{9,8},{10,9},{11,10},{12... | collective-permute-start | bytes 1572872 | tf_op jit(solution)/shard_map/ppermute | solution.py:570
  10.3 1.2 %copy-start = (f32[2,4,8,32,128]{4,3,2,1,0:T(8,128)S(1)}, f32[2,4,8,32,128]{4,3,2,1,0:T(8,128)}, u32[]{:S(2)}) copy-start(f32[2,4,8,32,128]{4,3,2,1,0:T(8,128)} %get-tuple-element.15.near_now) | copy-start | bytes 3145732
  11.5 1.2 %copy-start.1 = (f32[2,4,8,32,128]{4,3,2,1,0:T(8,128)S(1)}, f32[2,4,8,32,128]{4,3,2,1,0:T(8,128)}, u32[]{:S(2)}) copy-start(f32[2,4,8,32,128]{4,3,2,1,0:T(8,128)} %get-tuple-element.16.near_before) | copy-start | bytes 3145732
  12.7 18.4 %copy-start.2 = (f32[1280,128]{1,0:T(8,128)S(1)}, f32[1280,128]{1,0:T(8,128)}, u32[]{:S(2)}) copy-start(f32[1280,128]{1,0:T(8,128)} %get-tuple-element.14.base) | copy-start | bytes 1966084
  12.7 18.4 %copy-start.3 = (s32[128]{0:T(128)S(1)}, s32[128]{0:T(128)}, u32[]{:S(2)}) copy-start(s32[128]{0:T(128)} %tile_index.1) | copy-start | bytes 1540
  12.7 18.4 %copy-start.4 = (s32[128]{0:T(128)S(1)}, s32[128]{0:T(128)}, u32[]{:S(2)}) copy-start(s32[128]{0:T(128)} %step_offset.1) | copy-start | bytes 1540
  12.7 18.4 %copy-start.5 = (s32[128]{0:T(128)S(1)}, s32[128]{0:T(128)}, u32[]{:S(2)}) copy-start(s32[128]{0:T(128)} %get-tuple-element.13.place) | copy-start | bytes 1540
  14.9 16.2 %collective-permute-start.2 = (f32[4,2,144,128]{3,2,1,0:T(8,128)S(1)}, f32[4,2,144,128]{3,2,1,0:T(8,128)S(1)}, u32[]{:S(2)}, u32[]{:S(2)}) collective-permute-start(f32[4,2,144,128]{3,2,1,0:T(8,128)S(1)} %get-tuple-element.17), channel_id=1, source_target_pairs={{0,8},{8,16},{16,24},{1,9},{9,17},{17,25},{2,10},{10,18},{18,26},{... | collective-permute-start | bytes 1769480 | tf_op jit(solution)/shard_map/ppermute | solution.py:570
  18.7 12.4 %collective-permute-start.3 = (f32[4,2,144,128]{3,2,1,0:T(8,128)S(1)}, f32[4,2,144,128]{3,2,1,0:T(8,128)S(1)}, u32[]{:S(2)}, u32[]{:S(2)}) collective-permute-start(f32[4,2,144,128]{3,2,1,0:T(8,128)S(1)} %get-tuple-element.18), channel_id=1, source_target_pairs={{8,0},{16,8},{24,16},{9,1},{17,9},{25,17},{10,2},{18,10},{26,18},{... | collective-permute-start | bytes 1769480 | tf_op jit(solution)/shard_map/ppermute | solution.py:570
  31.2 28.5 %copy-start.6 = (s32[128,2]{0,1:T(2,128)S(1)}, s32[128,2]{0,1:T(2,128)}, u32[]{:S(2)}) copy-start(s32[128,2]{0,1:T(2,128)} %param.16) | copy-start | bytes 3076
  42.7 34.9 %all-to-all-start = ((f32[32,40,128]{2,1,0:T(8,128)}), f32[32,40,128]{2,1,0:T(8,128)S(1)}, u32[]{:S(2)}, u32[]{:S(2)}) async-start(f32[32,40,128]{2,1,0:T(8,128)} %bitcast), calls=%async_computation | async-start | bytes 1310720 | tf_op jit(solution)/shard_map/all_to_all | solution.py:643

commit v2 on v1

--- a/solution.py
+++ b/solution.py
@@ -80,11 +80,26 @@
         before[h, c, slot, top : top + STEPS, :] = y_high[c, x, STEPS:, z]
 
 
-def faces_kernel(near_now, near_before, y_low, y_high, out_low, out_high, p_now, p_before):
-    halves, comps, _, size_y, _ = near_now.shape
-    size_x = y_low.shape[1]
+def faces_kernel(now, before, y_low, y_high, _, out_low, out_high, p_now, p_before, sems):
+    comps, size_x, size_y, size_z = now.shape
+    halves = size_z // LANES
     rows = size_y + 2 * STEPS
     near = STEPS
+    copies = []
+    for a, (src, dst) in enumerate(((now, p_now), (before, p_before))):
+        for face in range(2):
+            x0 = 0 if face == 0 else size_x - near
+            s0 = 2 if face == 0 else 6
+            for h in range(halves):
+                copies.append(
+                    pltpu.make_async_copy(
+                        src.at[:, x0 : x0 + near, :, h * LANES : (h + 1) * LANES],
+                        dst.at[h, :, s0 : s0 + near, OWN : OWN + size_y, :],
+                        sems.at[a, face, h],
+                    )
+                )
+    for copy in copies:
+        copy.start()
 
     def slot(face, depth):
         return depth + 2 if face == 0 else 9 - depth
@@ -96,11 +111,6 @@
         for face in range(2):
             for depth in range(near):
                 x = depth if face == 0 else size_x - 1 - depth
-                place = depth if face == 0 else 2 * near - 1 - depth
-                for h in range(halves):
-                    own = slice(OWN, OWN + size_y)
-                    p_now[h, c, slot(face, depth), own, :] = near_now[h, c, place]
-                    p_before[h, c, slot(face, depth), own, :] = near_before[h, c, place]
                 fill_rows(p_now, p_before, c, slot(face, depth), y_low, y_high, x, size_y)
             for depth in (-1, -2):
                 for h in range(halves):
@@ -110,6 +120,8 @@
         return carry
 
     lax.fori_loop(0, comps, prepare, 0)
+    for copy in copies:
+        copy.wait()
 
     def give(buf, c, step, offset):
         more = STEPS - 1 - step
@@ -200,46 +212,19 @@
 
 
 SPREAD = 32
-GROUP = 8
+FETCH = 8
+GROUP = 32
 
 
 def panel_rows(lhs, weights, comps):
-    panels = []
-    height = comps * TILE
-    for b in range(0, len(lhs), 2):
-        left = jnp.concatenate([lhs[b], lhs[b + 1]], axis=0)
-        right = jnp.concatenate([weights[b], weights[b + 1]], axis=1)
-        made = jnp.dot(left, right, preferred_element_type=jnp.float32)
-        half = made.shape[1] // 2
-        for n, m in ((0, made[:height, :half]), (1, made[height:, half:])):
-            panels.append(
-                [
-                    jnp.sum(m[c * TILE : (c + 1) * TILE], axis=0, keepdims=True)
-                    for c in range(comps)
-                ]
-            )
-    return panels
-
-
-def place_kernel(
-    block_patch, ownership, now, before, out, place, near_now, near_before, count, sems,
-    *, slots, stride,
-):
-    comps, size_x, _, size_z = now.shape
-    copies = []
-    for a, (src, dst) in enumerate(((now, near_now), (before, near_before))):
-        for face in range(2):
-            x0 = 0 if face == 0 else size_x - STEPS
-            for h in range(size_z // LANES):
-                copies.append(
-                    pltpu.make_async_copy(
-                        src.at[:, x0 : x0 + STEPS, :, h * LANES : (h + 1) * LANES],
-                        dst.at[h, :, face * STEPS : (face + 1) * STEPS],
-                        sems.at[a, face, h],
-                    )
-                )
-    for copy in copies:
-        copy.start()
+    made = [jnp.dot(a, w, preferred_element_type=jnp.float32) for a, w in zip(lhs, weights)]
+    return [
+        [jnp.sum(m[c * TILE : (c + 1) * TILE], axis=0, keepdims=True) for c in range(comps)]
+        for m in made
+    ]
+
+
+def place_kernel(block_patch, ownership, out, place, count, *, comps, slots, stride):
     blocks = block_patch.shape[0]
     devices = lax.axis_size("bx") * lax.axis_size("by")
     owned = ownership.shape[0] // devices
@@ -250,6 +235,8 @@
         return carry
 
     lax.fori_loop(0, devices, clear, 0, unroll=8)
+
+    lane = lax.broadcasted_iota(jnp.int32, (1, LANES), 1)
 
     def one(b, carry):
         target = ownership[block_patch[b]]
@@ -259,15 +246,16 @@
         row = owner * stride + rank
         place[b] = row
         local = (target - owner * owned).astype(jnp.float32)
-        out[pl.ds(row + comps * slots, 1), :] = jnp.full((1, LANES), local, jnp.float32)
+        at = pl.ds(owner * stride + comps * slots, 1)
+        out[at, :] = jnp.where(lane == rank, local, out[at, :])
         return carry
 
     lax.fori_loop(0, blocks, one, 0, unroll=8)
-    for copy in copies:
-        copy.wait()
-
-
-def own_kernel(now, before, y_low, y_high, far, near, p_now, p_before, sems):
+
+
+def own_kernel(
+    now, before, y_low, y_high, weight, far, near, held, p_now, p_before, sems, wsems
+):
     comps, size_x, size_y, size_z = now.shape
     halves = size_z // LANES
     rows = size_y + 2 * STEPS
@@ -286,6 +274,15 @@
             )
     for copy in copies:
         copy.start()
+    blocks = weight.shape[0]
+    fetches = [
+        pltpu.make_async_copy(
+            weight.at[g * FETCH : (g + 1) * FETCH], held.at[g * FETCH : (g + 1) * FETCH], wsems.at[g]
+        )
+        for g in range(blocks // FETCH)
+    ]
+    for fetch in fetches:
+        fetch.start()
     edges = edge_rows()
     keep_low = lax.axis_index("bx") > 0
     keep_high = lax.axis_index("bx") < lax.axis_size("bx") - 1
@@ -346,26 +343,22 @@
                     h, :, x0 : x0 + STEPS, OWN : OWN + size_y, :
                 ]
         cur, old = old, cur
+    for fetch in fetches:
+        fetch.wait()
 
 
 def share_kernel(
-    tile_index, step_offset, place, base, from_low, from_high, far, near, weight, out,
-    bound, d_now, d_before, table, held, spread, lhs, wsems, *, slots,
+    tile_index, step_offset, place, base, from_low, from_high, far, near, held, out,
+    bound, d_now, d_before, table, spread, lhs, *, slots,
 ):
     _, halves, comps, _, size_y, _ = near.shape
     size_z = halves * LANES
     rows = size_y + 2 * STEPS
-    blocks = weight.shape[0]
+    blocks = held.shape[0]
     tiles_y = size_y // TILE
     tiles_z = size_z // TILE
     columns = 2 * tiles_y
 
-    def weights(g):
-        part = pl.ds(g * GROUP, GROUP)
-        return pltpu.make_async_copy(weight.at[part], held.at[part], wsems.at[g])
-
-    for g in range(blocks // GROUP):
-        weights(g).start()
     out[...] = base[...]
     edges = edge_rows()
     froms = (from_low, from_high)
@@ -438,7 +431,6 @@
         cur, old = old, cur
 
     def panels(g, carry):
-        weights(g).wait()
         made = panel_rows(
             [lhs[g * GROUP + b] for b in range(GROUP)],
             [held[g * GROUP + b] for b in range(GROUP)],
@@ -465,7 +457,7 @@
     lax.fori_loop(0, blocks // GROUP, panels, 0)
 
 
-PAIRS = 16
+PAIRS = 32
 
 
 def near_kernel(pairs, got, precorrection, out, field, total, held, sems, *, comps, slots, stride):
@@ -480,13 +472,28 @@
     for g in range(count // PAIRS):
         blocks(g).start()
     field[...] = jnp.zeros(field.shape, jnp.float32)
-    whole = got[...].reshape(senders, stride, LANES)
-    ids = whole[:, comps * slots : (comps + 1) * slots, :].reshape(senders * slots, LANES)
-    ids = ids.T[:owned]
-    hot = ids == lax.broadcasted_iota(jnp.int32, ids.shape, 0).astype(jnp.float32)
+    def rows_of(first, count):
+        return jnp.concatenate(
+            [got[n * stride + first : n * stride + first + count, :] for n in range(senders)],
+            axis=0,
+        )
+
+    wide = senders * slots
+    lane = lax.broadcasted_iota(jnp.int32, (LANES, wide), 0)
+    goal = lax.broadcasted_iota(jnp.int32, (LANES, wide), 1) % slots
+    pick = (lane == goal).astype(jnp.float32).astype(jnp.bfloat16)
+    ids = jnp.dot(
+        got[pl.ds(comps * slots, senders, stride=stride), :].astype(jnp.bfloat16),
+        pick,
+        preferred_element_type=jnp.float32,
+    )
+    sender = lax.broadcasted_iota(jnp.int32, ids.shape, 0)
+    goal = lax.broadcasted_iota(jnp.int32, ids.shape, 1) // slots
+    ids = jnp.sum(jnp.where(sender == goal, ids, 0.0), axis=0, keepdims=True)
+    hot = ids == lax.broadcasted_iota(jnp.int32, (owned, wide), 0).astype(jnp.float32)
     hot = hot.astype(jnp.float32).astype(jnp.bfloat16)
     for c in range(comps):
-        rest = whole[:, c * slots : (c + 1) * slots, :].reshape(senders * slots, LANES)
+        rest = rows_of(c * slots, slots)
         summed = None
         for _ in range(3):
             piece = rest.astype(jnp.bfloat16)
@@ -570,7 +577,7 @@
         return lax.ppermute(up, axis, forward), lax.ppermute(down, axis, backward)
 
     slots = ceil8(capacity)
-    stride = (comps + 1) * slots
+    stride = comps * slots + 1
     sent_shape = jax.ShapeDtypeStruct((devices * stride, points), f32)
 
     last, first = slice(size_y - STEPS, size_y), slice(0, STEPS)
@@ -579,17 +586,13 @@
     y_low, y_high = swap(up, down, "by", count_y)
 
     near_shape = jax.ShapeDtypeStruct((halves, comps, 2 * STEPS, size_y, LANES), f32)
-    base, place, near_now, near_before = pl.pallas_call(
-        functools.partial(place_kernel, slots=slots, stride=stride),
-        out_shape=(
-            sent_shape, jax.ShapeDtypeStruct((blocks,), jnp.int32), near_shape, near_shape
-        ),
-        in_specs=[SMEM, SMEM, HBM, HBM],
-        out_specs=(VMEM, SMEM, VMEM, VMEM),
-        scratch_shapes=[
-            pltpu.SMEM((devices,), jnp.int32), pltpu.SemaphoreType.DMA((2, 2, halves))
-        ],
-    )(block_patch, ownership, in_hbm(field_now), in_hbm(field_before))
+    base, place = pl.pallas_call(
+        functools.partial(place_kernel, comps=comps, slots=slots, stride=stride),
+        out_shape=(sent_shape, jax.ShapeDtypeStruct((blocks,), jnp.int32)),
+        in_specs=[SMEM, SMEM],
+        out_specs=(VMEM, SMEM),
+        scratch_shapes=[pltpu.SMEM((devices,), jnp.int32)],
+    )(block_patch, ownership)
 
     face_rows = STEPS * size_y + ceil8(STEPS * (STEPS - 1) + 4)
     face = jax.ShapeDtypeStruct((comps, halves, face_rows, LANES), f32)
@@ -597,51 +600,52 @@
     give_low, give_high = pl.pallas_call(
         faces_kernel,
         out_shape=(face, face),
-        in_specs=[VMEM, VMEM, VMEM, VMEM],
+        in_specs=[HBM, HBM, VMEM, VMEM, HBM],
         out_specs=(VMEM, VMEM),
-        scratch_shapes=[plane, plane],
+        scratch_shapes=[plane, plane, pltpu.SemaphoreType.DMA((2, 2, halves))],
         compiler_params=kernel_params(24),
-    )(near_now, near_before, y_low, y_high)
+    )(in_hbm(field_now), in_hbm(field_before), y_low, y_high, in_hbm(base))
     from_low, from_high = swap(give_high, give_low, "bx", count_x)
 
     tiles = size_x // TILE * (size_y // TILE) * (size_z // TILE)
     brick = pltpu.VMEM((halves, comps, size_x + 4, rows, LANES), f32)
     half = comps * STEPS * TILE
-    far, near = pl.pallas_call(
+    far, near, held = pl.pallas_call(
         own_kernel,
         out_shape=(
             jax.ShapeDtypeStruct((STEPS * tiles, TILE, half), f32),
-            jax.ShapeDtypeStruct((STEPS,) + near_shape.shape, f32),
+            jax.ShapeDtypeStruct((STEPS, halves, comps, 2 * STEPS, size_y, LANES), f32),
+            jax.ShapeDtypeStruct(interp_weight.shape, bf16),
         ),
-        in_specs=[HBM, HBM, VMEM, VMEM],
-        out_specs=(VMEM, VMEM),
-        scratch_shapes=[brick, brick, pltpu.SemaphoreType.DMA((2, halves))],
-        compiler_params=kernel_params(24),
-    )(in_hbm(field_now), in_hbm(field_before), y_low, y_high)
+        in_specs=[HBM, HBM, VMEM, VMEM, HBM],
+        out_specs=(VMEM, VMEM, VMEM),
+        scratch_shapes=[
+            brick,
+            brick,
+            pltpu.SemaphoreType.DMA((2, halves)),
+            pltpu.SemaphoreType.DMA((blocks // FETCH,)),
+        ],
+        compiler_params=kernel_params(18),
+    )(in_hbm(field_now), in_hbm(field_before), y_low, y_high, in_hbm(interp_weight))
 
     thin = pltpu.VMEM((halves, comps, 2 * STEPS, rows, LANES), f32)
     sent = pl.pallas_call(
         functools.partial(share_kernel, slots=slots),
         out_shape=sent_shape,
-        in_specs=[SMEM, SMEM, SMEM, VMEM, VMEM, VMEM, VMEM, VMEM, HBM],
+        in_specs=[SMEM, SMEM, SMEM, VMEM, VMEM, VMEM, VMEM, VMEM, VMEM],
         out_specs=VMEM,
         scratch_shapes=[
             thin,
             thin,
             thin,
             pltpu.VMEM((STEPS * tiles, TILE, half), f32),
-            pltpu.VMEM((blocks, cells, points), bf16),
             pltpu.VMEM((2 * half, comps * cells), bf16),
             pltpu.VMEM((blocks, comps * TILE, cells), bf16),
-            pltpu.SemaphoreType.DMA((blocks // GROUP,)),
         ],
-        compiler_params=kernel_params(40),
-    )(
-        tile_index, step_offset, place, base, from_low, from_high, far, near,
-        in_hbm(interp_weight),
-    )
+        compiler_params=kernel_params(20),
+    )(tile_index, step_offset, place, base, from_low, from_high, far, near, held)
     got = lax.all_to_all(
-        sent.reshape(devices, stride, points), ("bx", "by"), 0, 0, tiled=True
+        sent.reshape(devices, 1, stride * points), ("bx", "by"), 0, 0, tiled=True
     ).reshape(devices * stride, points)
 
     pairs = near_pairs.shape[0]

time: 82.3 us -> 76.1 us (0.925)
  local copies, waits for them, and re-layouts: 4.48 us -> 2.03 us
  Pallas kernels: 33 us -> 31 us
  starting transfers between devices: 25.7 us -> 24.8 us
    all_to_all x1, starting transfers between devices: 17 us -> 14 us  [per_device(): lax.all_to_all(sent.reshape(devices, 1, stride * points), ('bx', 'by'), 0...]
    unnamed x15 -> x11, local copies, waits for them, and re-layouts: 2.58 us -> 0.14 us
    all_to_all x1, waiting for transfers between devices: 17.7 us -> 15.6 us  [per_device(): lax.all_to_all(sent.reshape(devices, 1, stride * points), ('bx', 'by'), 0...]
    pallas_call x1, Pallas kernels: 11.4 us -> 9.42 us  [per_device(): pl.pallas_call(functools.partial(share_kernel, slots=slots), out_shape=se...]
    ppermute x4, starting transfers between devices: 8.76 us -> 10.7 us  [swap(): return (lax.ppermute(up, axis, forward), lax.ppermute(down, axis, backward))]
    ppermute x4, waiting for transfers between devices: 0.58 us -> 1.95 us  [swap(): return (lax.ppermute(up, axis, forward), lax.ppermute(down, axis, backward))]
  transfers between devices with their start and end apart: 5 -> 5, of which waited for: 2 -> 2; matrix products, arithmetic and copies ran while one was open for 0% -> 0% of each run, Pallas kernels for 18% -> 19%
where the time goes in v2:
time: 76.1 us; the launch traced here: 75.7 us
  Pallas kernels  31 us (41%)
  starting transfers between devices  24.8 us (33%)
  waiting for transfers between devices  17.5 us (23%)
  local copies, waits for them, and re-layouts  2.03 us (3%)
    all_to_all x1, waiting for transfers between devices, per_device(): lax.all_to_all(sent.reshape(devices, 1, stride * points), ('bx', 'by'), 0...  15.6 us
    all_to_all x1, starting transfers between devices, per_device(): lax.all_to_all(sent.reshape(devices, 1, stride * points), ('bx', 'by'), 0...  14 us
    pallas_call x1, Pallas kernels, per_device(): pl.pallas_call(own_kernel, out_shape=(jax.ShapeDtypeStruct((STEPS * tiles...  11.3 us
    ppermute x4, starting transfers between devices, swap(): return (lax.ppermute(up, axis, forward), lax.ppermute(down, axis, backward))  10.7 us
    pallas_call x1, Pallas kernels, per_device(): pl.pallas_call(functools.partial(share_kernel, slots=slots), out_shape=se...  9.42 us
    pallas_call x1, Pallas kernels, per_device(): pl.pallas_call(functools.partial(near_kernel, comps=comps, slots=slots, s...  3.98 us
    pallas_call x1, Pallas kernels, per_device(): pl.pallas_call(faces_kernel, out_shape=(face, face), in_specs=[HBM, HBM,...  3.5 us
    pallas_call x1, Pallas kernels, per_device(): pl.pallas_call(functools.partial(place_kernel, comps=comps, slots=slots,...  2.82 us
  transfers between devices with their start and end apart: 5, of which 2 were waited for; matrix products, arithmetic and copies ran while one was open for 0% of the time, Pallas kernels for 19%

profile of v2, /device:TPU:0, one launch (start us, length us, event | category | flops | bytes accessed | tf_op | source)
XLA Modules:
  0.0 75.7 jit_solution(3022604541865529251)
XLA Ops:
  0.0 1.8 %fusion = (f32[4,16,4,256]{3,2,1,0:T(4,128)S(1)}, f32[4,16,4,256]{3,2,1,0:T(4,128)S(1)}, f32[4,16,4,256]{3,2,1,0:T(4,128)S(1)}, f32[4,16,4,256]{3,2,1,0:T(4,128)S(1)}) fusion(f32[4,16,32,256]{3,2,1,0:T(8,128)} %now.3, f32[4,16,32,256]{3,2,1,0:T(8,128)} %before.3), kind=kLoop, calls=%fused_computation.2 | loop fusion | bytes 2097152 | tf_op jit(solution)/shard_map/slice | solution.py:585
  1.8 0.1 pad_maximum_fusion.1
  1.9 1.3 %collective-permute-start.1 = (f32[4,16,8,256]{3,2,1,0:T(8,128)S(1)}, f32[4,16,8,256]{3,2,1,0:T(8,128)S(1)}, u32[]{:S(2)}, u32[]{:S(2)}) collective-permute-start(f32[4,16,8,256]{3,2,1,0:T(8,128)S(1)} %pad_maximum_fusion.1), channel_id=1, source_target_pairs={{1,0},{2,1},{3,2},{4,3},{5,4},{6,5},{7,6},{9,8},{10,9},{11,10},{12... | collective-permute-start | bytes 1572872 | tf_op jit(solution)/shard_map/ppermute | solution.py:577
  3.2 0.1 pad_maximum_fusion
  3.3 3.1 %collective-permute-start = (f32[4,16,8,256]{3,2,1,0:T(8,128)S(1)}, f32[4,16,8,256]{3,2,1,0:T(8,128)S(1)}, u32[]{:S(2)}, u32[]{:S(2)}) collective-permute-start(f32[4,16,8,256]{3,2,1,0:T(8,128)S(1)} %pad_maximum_fusion), channel_id=1, source_target_pairs={{0,1},{1,2},{2,3},{3,4},{4,5},{5,6},{6,7},{8,9},{9,10},{10,11},{11... | collective-permute-start | bytes 1572872 | tf_op jit(solution)/shard_map/ppermute | solution.py:577
  6.4 2.8 %shard_map.91 = (f32[1056,128]{1,0:T(8,128)}, s32[128]{0:T(128)}) custom-call(s32[128]{0:T(128)} %block_patch.1, s32[2048]{0:T(1024)} %ownership.1), custom_call_target="tpu_custom_call" | custom-call | tf_op jit(solution)/shard_map/pallas_call | solution.py:589
  9.2 0.0 collective-permute-done.1.y_high
  9.2 0.0 collective-permute-done.y_low
  9.2 3.5 %shard_map.92 = (f32[4,2,144,128]{3,2,1,0:T(8,128)S(1)}, f32[4,2,144,128]{3,2,1,0:T(8,128)S(1)}) custom-call(f32[4,16,32,256]{3,2,1,0:T(8,128)} %now.3, f32[4,16,32,256]{3,2,1,0:T(8,128)} %before.3, f32[4,16,8,256]{3,2,1,0:T(8,128)S(1)} %collective-permute-done.y_low, f32[4,16,8,256]{3,2,1,0:T(8,128)S(1)} %collective-permute-done.1.y_high, ...), custom_call_target="tpu_custom_call" | custom-call | tf_op jit(solution)/shard_map/pallas_call | solution.py:600
  12.7 5.0 %collective-permute-start.2 = (f32[4,2,144,128]{3,2,1,0:T(8,128)S(1)}, f32[4,2,144,128]{3,2,1,0:T(8,128)S(1)}, u32[]{:S(2)}, u32[]{:S(2)}) collective-permute-start(f32[4,2,144,128]{3,2,1,0:T(8,128)S(1)} %get-tuple-element.14), channel_id=1, source_target_pairs={{0,8},{8,16},{16,24},{1,9},{9,17},{17,25},{2,10},{10,18},{18,26},{... | collective-permute-start | bytes 1769480 | tf_op jit(solution)/shard_map/ppermute | solution.py:577
  17.7 0.0 copy-start
  17.7 0.0 copy-start.1
  17.7 0.0 copy-start.2
  17.7 0.0 copy-start.3
  17.7 1.4 %collective-permute-start.3 = (f32[4,2,144,128]{3,2,1,0:T(8,128)S(1)}, f32[4,2,144,128]{3,2,1,0:T(8,128)S(1)}, u32[]{:S(2)}, u32[]{:S(2)}) collective-permute-start(f32[4,2,144,128]{3,2,1,0:T(8,128)S(1)} %get-tuple-element.15), channel_id=1, source_target_pairs={{8,0},{16,8},{24,16},{9,1},{17,9},{25,17},{10,2},{18,10},{26,18},{... | collective-permute-start | bytes 1769480 | tf_op jit(solution)/shard_map/ppermute | solution.py:577
  19.2 11.3 %shard_map.93 = (f32[1024,8,128]{2,1,0:T(8,128)S(1)}, f32[4,2,4,8,32,128]{5,4,3,2,1,0:T(8,128)S(1)}, bf16[128,512,128]{2,1,0:T(8,128)(2,1)S(1)}) custom-call(f32[4,16,32,256]{3,2,1,0:T(8,128)} %now.3, f32[4,16,32,256]{3,2,1,0:T(8,128)} %before.3, f32[4,16,8,256]{3,2,1,0:T(8,128)S(1)} %collective-permute-done.y_low, ...), custom_call_target="tpu_custom_call" | custom-call | tf_op jit(solution)/shard_map/pallas_call | solution.py:613
  30.5 0.0 collective-permute-done.2.from_low
  30.5 1.9 %collective-permute-done.3.from_high = f32[4,2,144,128]{3,2,1,0:T(8,128)S(1)} collective-permute-done((f32[4,2,144,128]{3,2,1,0:T(8,128)S(1)}, f32[4,2,144,128]{3,2,1,0:T(8,128)S(1)}, u32[]{:S(2)}, u32[]{:S(2)}) %collective-permute-start.3) | collective-permute-done | bytes 589856 | tf_op jit(solution)/shard_map/ppermute | solution.py:577
  32.4 0.0 copy-done
  32.4 0.0 copy-done.1
  32.4 0.0 copy-done.2
  32.4 0.0 copy-done.3
  32.4 0.0 copy-start.4
  32.4 9.4 %shard_map.94 = f32[1056,128]{1,0:T(8,128)} custom-call(s32[128]{0:T(128)S(1)} %copy-done.1, s32[128]{0:T(128)S(1)} %copy-done.2, s32[128]{0:T(128)S(1)} %copy-done.3, f32[1056,128]{1,0:T(8,128)S(1)} %copy-done, f32[4,2,144,128]{3,2,1,0:T(8,128)S(1)} %collective-permute-done.2.from_low, f32[4,2,144,128]{3,2,1,0:T(8,128)S(1)} %collective-permute-done.3.from_high, ...), custom_call_target="tpu_custom_call" | custom-call | tf_op jit(solution)/shard_map/pallas_call | solution.py:632
  41.9 14.0 %all-to-all-start = ((f32[32,1,4224]{2,1,0:T(1,128)}), f32[32,1,4224]{2,1,0:T(1,128)S(1)}, u32[]{:S(2)}, u32[]{:S(2)}) async-start(f32[32,1,4224]{2,1,0:T(1,128)} %bitcast), calls=%async_computation | async-start | bytes 1081344 | tf_op jit(solution)/shard_map/all_to_all | solution.py:647
  55.9 0.0 copy-done.4
  55.9 0.1 copy.11
  56.0 0.1 reshape.12.pairs
  56.2 15.6 %all-to-all-done = f32[32,1,4224]{2,1,0:T(1,128)S(1)} async-done(((f32[32,1,4224]{2,1,0:T(1,128)}), f32[32,1,4224]{2,1,0:T(1,128)S(1)}, u32[]{:S(2)}, u32[]{:S(2)}) %all-to-all-start) | async-done | bytes 540704 | tf_op jit(solution)/shard_map/all_to_all | solution.py:647
  71.7 4.0 %shard_map.95 = f32[256,128]{1,0:T(8,128)} custom-call(s32[256]{0:T(256)S(1)} %reshape.12.pairs, f32[1056,128]{1,0:T(8,128)S(1)} %bitcast.3, bf16[128,128,128]{2,1,0:T(8,128)(2,1)} %precorrection.1), custom_call_target="tpu_custom_call" | custom-call | tf_op jit(solution)/shard_map/pallas_call | solution.py:652
Async XLA Ops:
  1.9 7.3 %collective-permute-start.1 = (f32[4,16,8,256]{3,2,1,0:T(8,128)S(1)}, f32[4,16,8,256]{3,2,1,0:T(8,128)S(1)}, u32[]{:S(2)}, u32[]{:S(2)}) collective-permute-start(f32[4,16,8,256]{3,2,1,0:T(8,128)S(1)} %pad_maximum_fusion.1), channel_id=1, source_target_pairs={{1,0},{2,1},{3,2},{4,3},{5,4},{6,5},{7,6},{9,8},{10,9},{11,10},{12... | collective-permute-start | bytes 1572872 | tf_op jit(solution)/shard_map/ppermute | solution.py:577
  3.3 5.9 %collective-permute-start = (f32[4,16,8,256]{3,2,1,0:T(8,128)S(1)}, f32[4,16,8,256]{3,2,1,0:T(8,128)S(1)}, u32[]{:S(2)}, u32[]{:S(2)}) collective-permute-start(f32[4,16,8,256]{3,2,1,0:T(8,128)S(1)} %pad_maximum_fusion), channel_id=1, source_target_pairs={{0,1},{1,2},{2,3},{3,4},{4,5},{5,6},{6,7},{8,9},{9,10},{10,11},{11... | collective-permute-start | bytes 1572872 | tf_op jit(solution)/shard_map/ppermute | solution.py:577
  12.7 17.7 %collective-permute-start.2 = (f32[4,2,144,128]{3,2,1,0:T(8,128)S(1)}, f32[4,2,144,128]{3,2,1,0:T(8,128)S(1)}, u32[]{:S(2)}, u32[]{:S(2)}) collective-permute-start(f32[4,2,144,128]{3,2,1,0:T(8,128)S(1)} %get-tuple-element.14), channel_id=1, source_target_pairs={{0,8},{8,16},{16,24},{1,9},{9,17},{17,25},{2,10},{10,18},{18,26},{... | collective-permute-start | bytes 1769480 | tf_op jit(solution)/shard_map/ppermute | solution.py:577
  17.7 14.7 %copy-start = (f32[1056,128]{1,0:T(8,128)S(1)}, f32[1056,128]{1,0:T(8,128)}, u32[]{:S(2)}) copy-start(f32[1056,128]{1,0:T(8,128)} %get-tuple-element.13._.base) | copy-start | bytes 1622020
  17.7 14.7 %copy-start.1 = (s32[128]{0:T(128)S(1)}, s32[128]{0:T(128)}, u32[]{:S(2)}) copy-start(s32[128]{0:T(128)} %tile_index.1) | copy-start | bytes 1540
  17.7 14.7 %copy-start.2 = (s32[128]{0:T(128)S(1)}, s32[128]{0:T(128)}, u32[]{:S(2)}) copy-start(s32[128]{0:T(128)} %step_offset.1) | copy-start | bytes 1540
  17.7 14.7 %copy-start.3 = (s32[128]{0:T(128)S(1)}, s32[128]{0:T(128)}, u32[]{:S(2)}) copy-start(s32[128]{0:T(128)} %get-tuple-element.12.place) | copy-start | bytes 1540
  17.7 14.7 %collective-permute-start.3 = (f32[4,2,144,128]{3,2,1,0:T(8,128)S(1)}, f32[4,2,144,128]{3,2,1,0:T(8,128)S(1)}, u32[]{:S(2)}, u32[]{:S(2)}) collective-permute-start(f32[4,2,144,128]{3,2,1,0:T(8,128)S(1)} %get-tuple-element.15), channel_id=1, source_target_pairs={{8,0},{16,8},{24,16},{9,1},{17,9},{25,17},{10,2},{18,10},{26,18},{... | collective-permute-start | bytes 1769480 | tf_op jit(solution)/shard_map/ppermute | solution.py:577
  32.4 23.5 %copy-start.4 = (s32[128,2]{0,1:T(2,128)S(1)}, s32[128,2]{0,1:T(2,128)}, u32[]{:S(2)}) copy-start(s32[128,2]{0,1:T(2,128)} %param.16) | copy-start | bytes 3076
  41.9 29.9 %all-to-all-start = ((f32[32,1,4224]{2,1,0:T(1,128)}), f32[32,1,4224]{2,1,0:T(1,128)S(1)}, u32[]{:S(2)}, u32[]{:S(2)}) async-start(f32[32,1,4224]{2,1,0:T(1,128)} %bitcast), calls=%async_computation | async-start | bytes 1081344 | tf_op jit(solution)/shard_map/all_to_all | solution.py:647

commit v3 on v2

--- a/solution.py
+++ b/solution.py
@@ -80,7 +80,36 @@
         before[h, c, slot, top : top + STEPS, :] = y_high[c, x, STEPS:, z]
 
 
-def faces_kernel(now, before, y_low, y_high, _, out_low, out_high, p_now, p_before, sems):
+def pack_kernel(now, before, face_up, face_down, core_up, core_down, edge, sems):
+    comps, size_x, size_y, _ = now.shape
+    near = STEPS - 1
+    copies = []
+    for a, src in enumerate((now, before)):
+        for side, row in enumerate((0, size_y - TILE)):
+            copies.append(
+                pltpu.make_async_copy(
+                    src.at[:, :, row : row + TILE, :], edge.at[a, side], sems.at[a, side]
+                )
+            )
+    for copy in copies:
+        copy.start()
+    for copy in copies:
+        copy.wait()
+
+    def one(c, carry):
+        for side, face, core in ((0, face_down, core_down), (1, face_up, core_up)):
+            rows = slice(side * STEPS, (side + 1) * STEPS)
+            for a in range(2):
+                out = slice(a * STEPS, (a + 1) * STEPS)
+                face[c, :near, out, :] = edge[a, side, c, :near, rows, :]
+                face[c, near:, out, :] = edge[a, side, c, size_x - near :, rows, :]
+                core[c, :, out, :] = edge[a, side, c, near : size_x - near, rows, :]
+        return carry
+
+    lax.fori_loop(0, comps, one, 0)
+
+
+def faces_kernel(now, before, y_low, y_high, out_low, out_high, p_now, p_before, sems):
     comps, size_x, size_y, size_z = now.shape
     halves = size_z // LANES
     rows = size_y + 2 * STEPS
@@ -109,9 +138,14 @@
 
     def prepare(c, carry):
         for face in range(2):
-            for depth in range(near):
-                x = depth if face == 0 else size_x - 1 - depth
+            for depth in range(near - 1):
+                x = depth if face == 0 else 2 * (near - 1) - 1 - depth
                 fill_rows(p_now, p_before, c, slot(face, depth), y_low, y_high, x, size_y)
+            for h in range(halves):
+                zero = jnp.zeros((STEPS, LANES), jnp.float32)
+                for first in (OWN - STEPS, OWN + size_y):
+                    p_now[h, c, slot(face, near - 1), first : first + STEPS, :] = zero
+                    p_before[h, c, slot(face, near - 1), first : first + STEPS, :] = zero
             for depth in (-1, -2):
                 for h in range(halves):
                     zero = jnp.zeros((rows + 8, LANES), jnp.float32)
@@ -224,7 +258,7 @@
     ]
 
 
-def place_kernel(block_patch, ownership, out, place, count, *, comps, slots, stride):
+def place_kernel(block_patch, ownership, _, out, place, count, *, comps, slots, stride):
     blocks = block_patch.shape[0]
     devices = lax.axis_size("bx") * lax.axis_size("by")
     owned = ownership.shape[0] // devices
@@ -254,7 +288,8 @@
 
 
 def own_kernel(
-    now, before, y_low, y_high, weight, far, near, held, p_now, p_before, sems, wsems
+    now, before, face_low, face_high, core_low, core_high, weight, far, near, held,
+    p_now, p_before, sems, wsems,
 ):
     comps, size_x, size_y, size_z = now.shape
     halves = size_z // LANES
@@ -287,12 +322,17 @@
     keep_low = lax.axis_index("bx") > 0
     keep_high = lax.axis_index("bx") < lax.axis_size("bx") - 1
 
+    edge = STEPS - 1
+
     def prepare(c, carry):
         def one(x, carry):
-            fill_rows(p_now, p_before, c, x + 2, y_low, y_high, x, size_y)
+            fill_rows(p_now, p_before, c, x + 2 + edge, core_low, core_high, x, size_y)
             return carry
 
-        lax.fori_loop(0, size_x, one, 0)
+        lax.fori_loop(0, size_x - 2 * edge, one, 0)
+        for n in range(2 * edge):
+            x = n if n < edge else size_x - 2 * edge + n
+            fill_rows(p_now, p_before, c, x + 2, face_low, face_high, n, size_y)
         for place in (0, 1, size_x + 2, size_x + 3):
             for h in range(halves):
                 zero = jnp.zeros((rows + 8, LANES), jnp.float32)
@@ -580,19 +620,22 @@
     stride = comps * slots + 1
     sent_shape = jax.ShapeDtypeStruct((devices * stride, points), f32)
 
-    last, first = slice(size_y - STEPS, size_y), slice(0, STEPS)
-    up = jnp.concatenate([field_now[:, :, last], field_before[:, :, last]], axis=2)
-    down = jnp.concatenate([field_now[:, :, first], field_before[:, :, first]], axis=2)
-    y_low, y_high = swap(up, down, "by", count_y)
-
-    near_shape = jax.ShapeDtypeStruct((halves, comps, 2 * STEPS, size_y, LANES), f32)
-    base, place = pl.pallas_call(
-        functools.partial(place_kernel, comps=comps, slots=slots, stride=stride),
-        out_shape=(sent_shape, jax.ShapeDtypeStruct((blocks,), jnp.int32)),
-        in_specs=[SMEM, SMEM],
-        out_specs=(VMEM, SMEM),
-        scratch_shapes=[pltpu.SMEM((devices,), jnp.int32)],
-    )(block_patch, ownership)
+    edge = 2 * (STEPS - 1)
+    face_rim = jax.ShapeDtypeStruct((comps, edge, 2 * STEPS, size_z), f32)
+    core_rim = jax.ShapeDtypeStruct((comps, size_x - edge, 2 * STEPS, size_z), f32)
+    face_up, face_down, core_up, core_down = pl.pallas_call(
+        pack_kernel,
+        out_shape=(face_rim, face_rim, core_rim, core_rim),
+        in_specs=[HBM, HBM],
+        out_specs=(VMEM, VMEM, VMEM, VMEM),
+        scratch_shapes=[
+            pltpu.VMEM((2, 2, comps, size_x, TILE, size_z), f32),
+            pltpu.SemaphoreType.DMA((2, 2)),
+        ],
+        compiler_params=kernel_params(16),
+    )(in_hbm(field_now), in_hbm(field_before))
+    face_low, face_high = swap(face_up, face_down, "by", count_y)
+    core_low, core_high = swap(core_up, core_down, "by", count_y)
 
     face_rows = STEPS * size_y + ceil8(STEPS * (STEPS - 1) + 4)
     face = jax.ShapeDtypeStruct((comps, halves, face_rows, LANES), f32)
@@ -600,11 +643,21 @@
     give_low, give_high = pl.pallas_call(
         faces_kernel,
         out_shape=(face, face),
-        in_specs=[HBM, HBM, VMEM, VMEM, HBM],
+        in_specs=[HBM, HBM, VMEM, VMEM],
         out_specs=(VMEM, VMEM),
         scratch_shapes=[plane, plane, pltpu.SemaphoreType.DMA((2, 2, halves))],
+        cost_estimate=pl.CostEstimate(flops=5000000000, bytes_accessed=5000000, transcendentals=0),
         compiler_params=kernel_params(24),
-    )(in_hbm(field_now), in_hbm(field_before), y_low, y_high, in_hbm(base))
+    )(in_hbm(field_now), in_hbm(field_before), face_low, face_high)
+    base, place = pl.pallas_call(
+        functools.partial(place_kernel, comps=comps, slots=slots, stride=stride),
+        out_shape=(sent_shape, jax.ShapeDtypeStruct((blocks,), jnp.int32)),
+        in_specs=[SMEM, SMEM, HBM],
+        out_specs=(VMEM, SMEM),
+        scratch_shapes=[pltpu.SMEM((devices,), jnp.int32)],
+        cost_estimate=pl.CostEstimate(flops=10000000000, bytes_accessed=10000000, transcendentals=0),
+    )(block_patch, ownership, in_hbm(give_low))
+
     from_low, from_high = swap(give_high, give_low, "bx", count_x)
 
     tiles = size_x // TILE * (size_y // TILE) * (size_z // TILE)
@@ -617,7 +670,7 @@
             jax.ShapeDtypeStruct((STEPS, halves, comps, 2 * STEPS, size_y, LANES), f32),
             jax.ShapeDtypeStruct(interp_weight.shape, bf16),
         ),
-        in_specs=[HBM, HBM, VMEM, VMEM, HBM],
+        in_specs=[HBM, HBM, VMEM, VMEM, VMEM, VMEM, HBM],
         out_specs=(VMEM, VMEM, VMEM),
         scratch_shapes=[
             brick,
@@ -625,8 +678,12 @@
             pltpu.SemaphoreType.DMA((2, halves)),
             pltpu.SemaphoreType.DMA((blocks // FETCH,)),
         ],
+        cost_estimate=pl.CostEstimate(flops=20000000000, bytes_accessed=20000000, transcendentals=0),
         compiler_params=kernel_params(18),
-    )(in_hbm(field_now), in_hbm(field_before), y_low, y_high, in_hbm(interp_weight))
+    )(
+        in_hbm(field_now), in_hbm(field_before),
+        face_low, face_high, core_low, core_high, in_hbm(interp_weight),
+    )
 
     thin = pltpu.VMEM((halves, comps, 2 * STEPS, rows, LANES), f32)
     sent = pl.pallas_call(

time: 76.1 us -> 75.5 us (level)
  Pallas kernels: 31 us -> 33.8 us
  waiting for transfers between devices: 17.5 us -> 15.6 us
  local copies, waits for them, and re-layouts: 2.03 us -> 1.26 us
    all_to_all x1, starting transfers between devices: 14 us -> 8.13 us  [per_device(): lax.all_to_all(sent.reshape(devices, 1, stride * points), ('bx', 'by'), 0...]
    ppermute x4 -> x6, starting transfers between devices: 10.7 us -> 16 us  [swap(): return (lax.ppermute(up, axis, forward), lax.ppermute(down, axis, backward))]
    ppermute x4 -> x6, waiting for transfers between devices: 1.95 us -> 0.02 us  [swap(): return (lax.ppermute(up, axis, forward), lax.ppermute(down, axis, backward))]
    pallas_call x0 -> x1, Pallas kernels: none -> 1.77 us  [per_device(): pl.pallas_call(pack_kernel, out_shape=(face_rim, face_rim, core_rim, core...]
    slice x1 -> x0, local copies, waits for them, and re-layouts: 1.75 us -> none  [per_device(): field_now[:, :, first]]
    unnamed x11 -> x17, local copies, waits for them, and re-layouts: 0.14 us -> 1.12 us
    pallas_call x1, Pallas kernels: 11.3 us -> 12.2 us  [per_device(): pl.pallas_call(own_kernel, out_shape=(jax.ShapeDtypeStruct((STEPS * tiles...]
  transfers between devices with their start and end apart: 5 -> 7, of which waited for: 2 -> 1; matrix products, arithmetic and copies ran while one was open for 0% -> 0% of each run, Pallas kernels for 19% -> 25%
where the time goes in v3:
time: 75.5 us; the launch traced here: 75 us
  Pallas kernels  33.8 us (45%)
  starting transfers between devices  24.1 us (32%)
  waiting for transfers between devices  15.6 us (21%)
  local copies, waits for them, and re-layouts  1.26 us (2%)
    ppermute x6, starting transfers between devices, swap(): return (lax.ppermute(up, axis, forward), lax.ppermute(down, axis, backward))  16 us
    all_to_all x1, waiting for transfers between devices, per_device(): lax.all_to_all(sent.reshape(devices, 1, stride * points), ('bx', 'by'), 0...  15.6 us
    pallas_call x1, Pallas kernels, per_device(): pl.pallas_call(own_kernel, out_shape=(jax.ShapeDtypeStruct((STEPS * tiles...  12.2 us
    pallas_call x1, Pallas kernels, per_device(): pl.pallas_call(functools.partial(share_kernel, slots=slots), out_shape=se...  9.45 us
    all_to_all x1, starting transfers between devices, per_device(): lax.all_to_all(sent.reshape(devices, 1, stride * points), ('bx', 'by'), 0...  8.13 us
    pallas_call x1, Pallas kernels, per_device(): pl.pallas_call(functools.partial(near_kernel, comps=comps, slots=slots, s...  3.98 us
    pallas_call x1, Pallas kernels, per_device(): pl.pallas_call(faces_kernel, out_shape=(face, face), in_specs=[HBM, HBM,...  3.56 us
    pallas_call x1, Pallas kernels, per_device(): pl.pallas_call(functools.partial(place_kernel, comps=comps, slots=slots,...  2.84 us
  transfers between devices with their start and end apart: 7, of which 1 were waited for; matrix products, arithmetic and copies ran while one was open for 0% of the time, Pallas kernels for 25%

profile of v3, /device:TPU:0, one launch (start us, length us, event | category | flops | bytes accessed | tf_op | source)
XLA Modules:
  0.0 75.0 jit_solution(1513708374237102353)
XLA Ops:
  0.0 1.8 %shard_map.91 = (f32[4,6,8,256]{3,2,1,0:T(8,128)S(1)}, f32[4,6,8,256]{3,2,1,0:T(8,128)S(1)}, f32[4,10,8,256]{3,2,1,0:T(8,128)S(1)}, f32[4,10,8,256]{3,2,1,0:T(8,128)S(1)}) custom-call(f32[4,16,32,256]{3,2,1,0:T(8,128)} %now.5, f32[4,16,32,256]{3,2,1,0:T(8,128)} %before.5), custom_call_target="tpu_custom_call" | custom-call | tf_op jit(solution)/shard_map/pallas_call | solution.py:626
  1.8 2.4 %collective-permute-start = (f32[4,6,8,256]{3,2,1,0:T(8,128)S(1)}, f32[4,6,8,256]{3,2,1,0:T(8,128)S(1)}, u32[]{:S(2)}, u32[]{:S(2)}) collective-permute-start(f32[4,6,8,256]{3,2,1,0:T(8,128)S(1)} %get-tuple-element.16), channel_id=1, source_target_pairs={{0,1},{1,2},{2,3},{3,4},{4,5},{5,6},{6,7},{8,9},{9,10},{10,11},{11... | collective-permute-start | bytes 589832 | tf_op jit(solution)/shard_map/ppermute | solution.py:617
  4.2 1.3 %collective-permute-start.1 = (f32[4,6,8,256]{3,2,1,0:T(8,128)S(1)}, f32[4,6,8,256]{3,2,1,0:T(8,128)S(1)}, u32[]{:S(2)}, u32[]{:S(2)}) collective-permute-start(f32[4,6,8,256]{3,2,1,0:T(8,128)S(1)} %get-tuple-element.17), channel_id=1, source_target_pairs={{1,0},{2,1},{3,2},{4,3},{5,4},{6,5},{7,6},{9,8},{10,9},{11,10},{12... | collective-permute-start | bytes 589832 | tf_op jit(solution)/shard_map/ppermute | solution.py:617
  5.5 5.1 %collective-permute-start.4 = (f32[4,10,8,256]{3,2,1,0:T(8,128)S(1)}, f32[4,10,8,256]{3,2,1,0:T(8,128)S(1)}, u32[]{:S(2)}, u32[]{:S(2)}) collective-permute-start(f32[4,10,8,256]{3,2,1,0:T(8,128)S(1)} %get-tuple-element.22), channel_id=1, source_target_pairs={{0,1},{1,2},{2,3},{3,4},{4,5},{5,6},{6,7},{8,9},{9,10},{10,11},{11... | collective-permute-start | bytes 983048 | tf_op jit(solution)/shard_map/ppermute | solution.py:617
  10.6 1.3 %collective-permute-start.5 = (f32[4,10,8,256]{3,2,1,0:T(8,128)S(1)}, f32[4,10,8,256]{3,2,1,0:T(8,128)}, u32[]{:S(2)}, u32[]{:S(2)}) collective-permute-start(f32[4,10,8,256]{3,2,1,0:T(8,128)S(1)} %get-tuple-element.23), channel_id=1, source_target_pairs={{1,0},{2,1},{3,2},{4,3},{5,4},{6,5},{7,6},{9,8},{10,9},{11,10},{12... | collective-permute-start | bytes 983048 | tf_op jit(solution)/shard_map/ppermute | solution.py:617
  11.9 0.0 collective-permute-done.y_low.face_low
  11.9 0.0 collective-permute-done.1.y_high.face_high
  11.9 0.0 copy-start.5
  11.9 3.6 %shard_map.92 = (f32[4,2,144,128]{3,2,1,0:T(8,128)S(1)}, f32[4,2,144,128]{3,2,1,0:T(8,128)S(1)}) custom-call(f32[4,16,32,256]{3,2,1,0:T(8,128)} %now.5, f32[4,16,32,256]{3,2,1,0:T(8,128)} %before.5, f32[4,6,8,256]{3,2,1,0:T(8,128)S(1)} %collective-permute-done.y_low.face_low, f32[4,6,8,256]{3,2,1,0:T(8,128)S(1)} %collective-permute-done.1.y_high.face_high), custom_call_target="tpu_custom_call" | custom-call | flops 5000000000 | bytes 5000000 | tf_op jit(solution)/shard_map/pallas_call | solution.py:643
  15.5 0.0 copy-done.5
  15.5 0.0 copy-start.4
  15.5 1.3 %collective-permute-start.3 = (f32[4,2,144,128]{3,2,1,0:T(8,128)S(1)}, f32[4,2,144,128]{3,2,1,0:T(8,128)S(1)}, u32[]{:S(2)}, u32[]{:S(2)}) collective-permute-start(f32[4,2,144,128]{3,2,1,0:T(8,128)S(1)} %get-tuple-element.18._), channel_id=1, source_target_pairs={{8,0},{16,8},{24,16},{9,1},{17,9},{25,17},{10,2},{18,10},{26,18},{... | collective-permute-start | bytes 1769480 | tf_op jit(solution)/shard_map/ppermute | solution.py:617
  16.8 4.6 %collective-permute-start.2 = (f32[4,2,144,128]{3,2,1,0:T(8,128)S(1)}, f32[4,2,144,128]{3,2,1,0:T(8,128)S(1)}, u32[]{:S(2)}, u32[]{:S(2)}) collective-permute-start(f32[4,2,144,128]{3,2,1,0:T(8,128)S(1)} %get-tuple-element.21), channel_id=1, source_target_pairs={{0,8},{8,16},{16,24},{1,9},{9,17},{17,25},{2,10},{10,18},{18,26},{... | collective-permute-start | bytes 1769480 | tf_op jit(solution)/shard_map/ppermute | solution.py:617
  21.4 0.0 copy-done.4
  21.4 2.8 %shard_map.93 = (f32[1056,128]{1,0:T(8,128)}, s32[128]{0:T(128)}) custom-call(s32[128]{0:T(128)} %block_patch.1, s32[2048]{0:T(1024)} %ownership.1, f32[4,2,144,128]{3,2,1,0:T(8,128)} %copy-done.4), custom_call_target="tpu_custom_call" | custom-call | flops 10000000000 | bytes 10000000 | tf_op jit(solution)/shard_map/pallas_call | solution.py:652
  24.3 0.0 copy-start
  24.3 0.0 copy-start.1
  24.3 0.0 copy-start.2
  24.3 0.0 copy-start.3
  24.3 0.0 collective-permute-done.4.core_low
  24.3 0.0 collective-permute-done.5.core_high
  24.4 1.0 %copy-done.6 = f32[4,6,8,256]{3,2,1,0:T(8,128)S(1)} copy-done((f32[4,6,8,256]{3,2,1,0:T(8,128)S(1)}, f32[4,6,8,256]{3,2,1,0:T(8,128)}, u32[]{:S(2)}) %copy-start.6) | copy-done | bytes 196632
  25.3 12.2 %shard_map.94 = (f32[1024,8,128]{2,1,0:T(8,128)S(1)}, f32[4,2,4,8,32,128]{5,4,3,2,1,0:T(8,128)S(1)}, bf16[128,512,128]{2,1,0:T(8,128)(2,1)S(1)}) custom-call(f32[4,16,32,256]{3,2,1,0:T(8,128)} %now.5, f32[4,16,32,256]{3,2,1,0:T(8,128)} %before.5, f32[4,6,8,256]{3,2,1,0:T(8,128)S(1)} %collective-permute-done.y_low.face_low, f32[4,6,8,256]{3,2,1,0:T(8,128)S(1)} %copy-done.6, ...), custom_call_target="tpu_custom_call" | custom-call | flops 20000000000 | bytes 20000000 | tf_op jit(solution)/shard_map/pallas_call | solution.py:666
  37.6 0.0 collective-permute-done.3.from_high
  37.6 0.0 collective-permute-done.2.from_low
  37.6 0.0 copy-start.7
  37.6 9.4 %shard_map.95 = f32[1056,128]{1,0:T(8,128)} custom-call(s32[128]{0:T(128)S(1)} %copy-done.1, s32[128]{0:T(128)S(1)} %copy-done.2, s32[128]{0:T(128)S(1)} %copy-done.3, f32[1056,128]{1,0:T(8,128)S(1)} %copy-done, f32[4,2,144,128]{3,2,1,0:T(8,128)S(1)} %collective-permute-done.2.from_low, f32[4,2,144,128]{3,2,1,0:T(8,128)S(1)} %collective-permute-done.3.from_high, ...), custom_call_target="tpu_custom_call" | custom-call | tf_op jit(solution)/shard_map/pallas_call | solution.py:689
  47.1 8.1 %all-to-all-start = ((f32[32,1,4224]{2,1,0:T(1,128)}), f32[32,1,4224]{2,1,0:T(1,128)S(1)}, u32[]{:S(2)}, u32[]{:S(2)}) async-start(f32[32,1,4224]{2,1,0:T(1,128)} %bitcast), calls=%async_computation | async-start | bytes 1081344 | tf_op jit(solution)/shard_map/all_to_all | solution.py:704
  55.2 0.1 copy.11
  55.3 0.1 reshape.12.pairs
  55.5 15.6 %all-to-all-done = f32[32,1,4224]{2,1,0:T(1,128)S(1)} async-done(((f32[32,1,4224]{2,1,0:T(1,128)}), f32[32,1,4224]{2,1,0:T(1,128)S(1)}, u32[]{:S(2)}, u32[]{:S(2)}) %all-to-all-start) | async-done | bytes 540704 | tf_op jit(solution)/shard_map/all_to_all | solution.py:704
  71.0 4.0 %shard_map.96 = f32[256,128]{1,0:T(8,128)} custom-call(s32[256]{0:T(256)S(1)} %reshape.12.pairs, f32[1056,128]{1,0:T(8,128)S(1)} %bitcast.3, bf16[128,128,128]{2,1,0:T(8,128)(2,1)} %precorrection.1), custom_call_target="tpu_custom_call" | custom-call | tf_op jit(solution)/shard_map/pallas_call | solution.py:709
  (6 shorter events, 0.0 us)
Async XLA Ops:
  1.8 10.1 %collective-permute-start = (f32[4,6,8,256]{3,2,1,0:T(8,128)S(1)}, f32[4,6,8,256]{3,2,1,0:T(8,128)S(1)}, u32[]{:S(2)}, u32[]{:S(2)}) collective-permute-start(f32[4,6,8,256]{3,2,1,0:T(8,128)S(1)} %get-tuple-element.16), channel_id=1, source_target_pairs={{0,1},{1,2},{2,3},{3,4},{4,5},{5,6},{6,7},{8,9},{9,10},{10,11},{11... | collective-permute-start | bytes 589832 | tf_op jit(solution)/shard_map/ppermute | solution.py:617
  4.2 7.8 %collective-permute-start.1 = (f32[4,6,8,256]{3,2,1,0:T(8,128)S(1)}, f32[4,6,8,256]{3,2,1,0:T(8,128)S(1)}, u32[]{:S(2)}, u32[]{:S(2)}) collective-permute-start(f32[4,6,8,256]{3,2,1,0:T(8,128)S(1)} %get-tuple-element.17), channel_id=1, source_target_pairs={{1,0},{2,1},{3,2},{4,3},{5,4},{6,5},{7,6},{9,8},{10,9},{11,10},{12... | collective-permute-start | bytes 589832 | tf_op jit(solution)/shard_map/ppermute | solution.py:617
  5.5 18.9 %collective-permute-start.4 = (f32[4,10,8,256]{3,2,1,0:T(8,128)S(1)}, f32[4,10,8,256]{3,2,1,0:T(8,128)S(1)}, u32[]{:S(2)}, u32[]{:S(2)}) collective-permute-start(f32[4,10,8,256]{3,2,1,0:T(8,128)S(1)} %get-tuple-element.22), channel_id=1, source_target_pairs={{0,1},{1,2},{2,3},{3,4},{4,5},{5,6},{6,7},{8,9},{9,10},{10,11},{11... | collective-permute-start | bytes 983048 | tf_op jit(solution)/shard_map/ppermute | solution.py:617
  10.6 13.7 %collective-permute-start.5 = (f32[4,10,8,256]{3,2,1,0:T(8,128)S(1)}, f32[4,10,8,256]{3,2,1,0:T(8,128)}, u32[]{:S(2)}, u32[]{:S(2)}) collective-permute-start(f32[4,10,8,256]{3,2,1,0:T(8,128)S(1)} %get-tuple-element.23), channel_id=1, source_target_pairs={{1,0},{2,1},{3,2},{4,3},{5,4},{6,5},{7,6},{9,8},{10,9},{11,10},{12... | collective-permute-start | bytes 983048 | tf_op jit(solution)/shard_map/ppermute | solution.py:617
  11.9 3.6 %copy-start.5 = (f32[4,6,8,256]{3,2,1,0:T(8,128)}, f32[4,6,8,256]{3,2,1,0:T(8,128)S(1)}, u32[]{:S(2)}) copy-start(f32[4,6,8,256]{3,2,1,0:T(8,128)S(1)} %collective-permute-done.1.y_high.face_high) | copy-start | bytes 589828
  15.5 5.9 %copy-start.4 = (f32[4,2,144,128]{3,2,1,0:T(8,128)}, f32[4,2,144,128]{3,2,1,0:T(8,128)S(1)}, u32[]{:S(2)}) copy-start(f32[4,2,144,128]{3,2,1,0:T(8,128)S(1)} %get-tuple-element.18._) | copy-start | bytes 1769476
  15.5 22.0 %collective-permute-start.3 = (f32[4,2,144,128]{3,2,1,0:T(8,128)S(1)}, f32[4,2,144,128]{3,2,1,0:T(8,128)S(1)}, u32[]{:S(2)}, u32[]{:S(2)}) collective-permute-start(f32[4,2,144,128]{3,2,1,0:T(8,128)S(1)} %get-tuple-element.18._), channel_id=1, source_target_pairs={{8,0},{16,8},{24,16},{9,1},{17,9},{25,17},{10,2},{18,10},{26,18},{... | collective-permute-start | bytes 1769480 | tf_op jit(solution)/shard_map/ppermute | solution.py:617
  16.8 20.7 %collective-permute-start.2 = (f32[4,2,144,128]{3,2,1,0:T(8,128)S(1)}, f32[4,2,144,128]{3,2,1,0:T(8,128)S(1)}, u32[]{:S(2)}, u32[]{:S(2)}) collective-permute-start(f32[4,2,144,128]{3,2,1,0:T(8,128)S(1)} %get-tuple-element.21), channel_id=1, source_target_pairs={{0,8},{8,16},{16,24},{1,9},{9,17},{17,25},{2,10},{10,18},{18,26},{... | collective-permute-start | bytes 1769480 | tf_op jit(solution)/shard_map/ppermute | solution.py:617
  24.3 13.3 %copy-start = (f32[1056,128]{1,0:T(8,128)S(1)}, f32[1056,128]{1,0:T(8,128)}, u32[]{:S(2)}) copy-start(f32[1056,128]{1,0:T(8,128)} %get-tuple-element.20.base) | copy-start | bytes 1622020
  24.3 13.3 %copy-start.1 = (s32[128]{0:T(128)S(1)}, s32[128]{0:T(128)}, u32[]{:S(2)}) copy-start(s32[128]{0:T(128)} %tile_index.1) | copy-start | bytes 1540
  24.3 13.3 %copy-start.2 = (s32[128]{0:T(128)S(1)}, s32[128]{0:T(128)}, u32[]{:S(2)}) copy-start(s32[128]{0:T(128)} %step_offset.1) | copy-start | bytes 1540
  24.3 13.3 %copy-start.3 = (s32[128]{0:T(128)S(1)}, s32[128]{0:T(128)}, u32[]{:S(2)}) copy-start(s32[128]{0:T(128)} %get-tuple-element.19.place) | copy-start | bytes 1540
  24.3 1.0 %copy-start.6 = (f32[4,6,8,256]{3,2,1,0:T(8,128)S(1)}, f32[4,6,8,256]{3,2,1,0:T(8,128)}, u32[]{:S(2)}) copy-start(f32[4,6,8,256]{3,2,1,0:T(8,128)} %copy-done.5) | copy-start | bytes 589828
  37.6 17.6 %copy-start.7 = (s32[128,2]{0,1:T(2,128)S(1)}, s32[128,2]{0,1:T(2,128)}, u32[]{:S(2)}) copy-start(s32[128,2]{0,1:T(2,128)} %param.16) | copy-start | bytes 3076
  47.1 24.0 %all-to-all-start = ((f32[32,1,4224]{2,1,0:T(1,128)}), f32[32,1,4224]{2,1,0:T(1,128)S(1)}, u32[]{:S(2)}, u32[]{:S(2)}) async-start(f32[32,1,4224]{2,1,0:T(1,128)} %bitcast), calls=%async_computation | async-start | bytes 1081344 | tf_op jit(solution)/shard_map/all_to_all | solution.py:704
